TPU v7x, 512 devices: a whole 4x4x16 slice. The times are simulated.
512 devices in a mesh: clu: 32 (over y, x, core), col: 16 (over z).
Axes of the slice: x: 4, y: 4, z: 16, core: 2. Of those that a mesh axis runs over, the one named last changes fastest.
Arguments:
- positions: float32 [16384, 2, 128], P(('clu', 'col')), may hold values from -4 to 4
- tension: float32 [16384, 128], P(('clu', 'col')), may hold values from -6 to 6
- bending: float32 [16384], P(('clu', 'col')), may hold values from 0.3 to 3
- moved_order: int32 [512, 32], P(('clu', 'col')), may hold values from 0 to 31, each once within a row
- move_destination: int32 [12288, 1], P(('clu', 'col')), may hold values from 0 to 31; in each aligned block of 24 rows (0 to 23, 24 to 47, ...) at most 2 rows name the same one
- move_target: int32 [12288], P(('clu', 'col')), may hold values from 0 to 31
- far_range: int32 [16384, 1], P(('clu', 'col')), may hold values from 0 to 15; in each aligned block of 32 rows (0 to 31, 32 to 63, ...) at most 4 rows name the same one
- old_basis: bfloat16 [128, 8192], P(None, 'col'), may hold values from -6 to 6
- source_nodes: bfloat16 [2, 8192], P(None, 'col'), may hold values from -4 to 4
Outputs:
- force: float32 [16384, 2, 128], P(('clu', 'col'))
- near_velocity: float32 [16384, 2, 128], P(('clu', 'col'))
- new_basis: float32 [16384, 64, 2, 128], P(('clu', 'col'))
Inputs may be any that keep to these rules, and one draw needn't show every extreme that they name: `moved_order`: each row of a device lists its 32 vesicles once each; the first 24 are the moved ones. `move_destination`: among the 24 rows of one device no cluster is named more than 2 times. `far_range`: among the 32 rows of one device no column range is named more than 4 times.
All inputs are finite; a program needn't handle non-finite values.
Results may differ from a plain program's by a relative error of at most 0.0045.
Values may be sent and summed in bfloat16 or wider, within the bound.
A program may use at most 64 MiB of HBM per device.

v0:
```python
import math

import jax
import jax.numpy as jnp
from jax import lax
from jax.sharding import PartitionSpec as P

EPS_SQUARED = 0.01


def spectral_tables(node_count):
    half_count = node_count // 2
    node_index = lax.broadcasted_iota(jnp.int32, (node_count, half_count + 1), 0)
    wave_index = lax.broadcasted_iota(jnp.int32, (node_count, half_count + 1), 1)
    phase_angle = (node_index * wave_index % node_count).astype(jnp.float32) * (
        2.0 * math.pi / node_count
    )
    cosine_table = jnp.cos(phase_angle)
    sine_table = jnp.sin(phase_angle)
    wavenumber = lax.broadcasted_iota(jnp.int32, (half_count + 1,), 0).astype(jnp.float32)
    inside = jnp.logical_and(wavenumber > 0, wavenumber < half_count)
    first_weight = jnp.where(inside, 2.0 * wavenumber / half_count, 0.0)
    fourth_weight = jnp.where(
        inside, 2.0 * (wavenumber / half_count) ** 4, jnp.where(wavenumber == half_count, 1.0, 0.0)
    )
    highest = lax.Precision.HIGHEST
    derivative = (
        jnp.dot(cosine_table * first_weight, sine_table.T, precision=highest)
        - jnp.dot(sine_table * first_weight, cosine_table.T, precision=highest)
    ) / node_count
    bending_table = (
        jnp.dot(cosine_table * fourth_weight, cosine_table.T, precision=highest)
        + jnp.dot(sine_table * fourth_weight, sine_table.T, precision=highest)
    ) / node_count
    return (derivative, bending_table)


def membrane_force(positions, tension, bending, derivative, bending_table):
    vesicles, node_count = (positions.shape[0], positions.shape[2])
    highest = lax.Precision.HIGHEST
    flat_rows = positions.reshape(vesicles * 2, node_count)
    slope = jnp.dot(flat_rows, derivative.T, precision=highest).reshape(vesicles, 2, node_count)
    fourth = jnp.dot(flat_rows, bending_table.T, precision=highest).reshape(vesicles, 2, node_count)
    pulled = (tension[:, None, :] * slope).reshape(vesicles * 2, node_count)
    tension_part = jnp.dot(pulled, derivative.T, precision=highest).reshape(vesicles, 2, node_count)
    return tension_part - bending[:, None, None] * fourth


def near_velocity_block(target_nodes, source_nodes, source_force):
    delta_x = target_nodes[0][:, None] - source_nodes[0][None, :]
    delta_y = target_nodes[1][:, None] - source_nodes[1][None, :]
    spread = delta_x * delta_x + delta_y * delta_y + EPS_SQUARED
    log_part = -0.5 * jnp.log(spread)
    push_x = source_force[0][None, :]
    push_y = source_force[1][None, :]
    along = (delta_x * push_x + delta_y * push_y) / spread
    speed_x = jnp.sum(log_part * push_x + delta_x * along, axis=1)
    speed_y = jnp.sum(log_part * push_y + delta_y * along, axis=1)
    return jnp.stack([speed_x, speed_y]) / target_nodes.shape[1]


def far_kernel(targets, sources):
    delta_x = targets[..., 0, None, :] - sources[..., 0, :, None]
    delta_y = targets[..., 1, None, :] - sources[..., 1, :, None]
    spread = delta_x * delta_x + delta_y * delta_y + EPS_SQUARED
    log_part = -0.5 * jnp.log(spread)
    first_first = log_part + delta_x * delta_x / spread
    first_second = delta_x * delta_y / spread
    second_second = log_part + delta_y * delta_y / spread
    upper_rows = jnp.stack([first_first, first_second], axis=-3)
    lower_rows = jnp.stack([first_second, second_second], axis=-3)
    return jnp.stack([upper_rows, lower_rows], axis=-4).astype(jnp.bfloat16)


def group_size():
    return 4


def earlier_count(hot_table):
    return jnp.sum((jnp.cumsum(hot_table, axis=0) - hot_table) * hot_table, axis=1)


def per_device(
    positions,
    tension,
    bending,
    moved_order,
    move_destination,
    move_target,
    far_range,
    old_basis,
    source_nodes,
):
    highest = lax.Precision.HIGHEST
    vesicles, node_count = (positions.shape[0], positions.shape[2])
    rank_count = old_basis.shape[0] // 2
    source_count = old_basis.shape[1]
    derivative, bending_table = spectral_tables(node_count)
    force = membrane_force(positions, tension, bending, derivative, bending_table)
    clu_count = lax.axis_size("clu")
    move_count = move_target.shape[0]
    slot_cap = 2 * ((move_count + clu_count - 1) // clu_count)
    order_row = moved_order[0, :move_count]
    pick_table = (
        order_row[:, None] == lax.broadcasted_iota(jnp.int32, (move_count, vesicles), 1)
    ).astype(jnp.float32)
    carried = jnp.concatenate([positions, force], axis=1).reshape(vesicles, 4 * node_count)
    moving = jnp.dot(pick_table, carried, precision=highest)
    destination = move_destination[:, 0]
    dest_hot = (
        destination[:, None] == lax.broadcasted_iota(jnp.int32, (move_count, clu_count), 1)
    ).astype(jnp.int32)
    slot_index = destination * slot_cap + earlier_count(dest_hot)
    slot_total = clu_count * slot_cap
    pack_table = (
        slot_index[None, :] == lax.broadcasted_iota(jnp.int32, (slot_total, move_count), 0)
    ).astype(jnp.float32)
    packed = jnp.dot(pack_table, moving, precision=highest).reshape(
        clu_count, slot_cap, 4, node_count
    )
    target_tag = jnp.dot(
        pack_table, (move_target + 1).astype(jnp.float32), precision=highest
    ).reshape(clu_count, slot_cap)
    arrived, arrived_tag = (
        lax.all_to_all(packed, "clu", split_axis=0, concat_axis=0, tiled=True),
        lax.all_to_all(target_tag, "clu", split_axis=0, concat_axis=0, tiled=True),
    )
    arrived = arrived.reshape(slot_total, 4, node_count)
    arrived_tag = arrived_tag.reshape(slot_total)
    target_hot = (
        arrived_tag[:, None]
        == (lax.broadcasted_iota(jnp.int32, (slot_total, vesicles), 1) + 1).astype(jnp.float32)
    ).astype(jnp.float32)
    target_nodes = jnp.dot(
        target_hot, positions.reshape(vesicles, 2 * node_count), precision=highest
    ).reshape(slot_total, 2, node_count)
    near_width = group_size()

    def near_group(pieces):
        targets, sources = pieces
        return jax.vmap(near_velocity_block)(targets, sources[:, 0:2], sources[:, 2:4])

    speeds = lax.map(
        near_group,
        (
            target_nodes.reshape(-1, near_width, 2, node_count),
            arrived.reshape(-1, near_width, 4, node_count),
        ),
    )
    speeds = speeds.reshape(slot_total, 2 * node_count)
    near_velocity = jnp.dot(target_hot.T, speeds, precision=highest).reshape(
        vesicles, 2, node_count
    )
    chosen = far_range[:, 0]
    col_count = lax.axis_size("col")
    capacity = 2 * ((vesicles + col_count - 1) // col_count)
    range_hot = (
        chosen[:, None] == lax.broadcasted_iota(jnp.int32, (vesicles, col_count), 1)
    ).astype(jnp.int32)
    place_index = chosen * capacity + earlier_count(range_hot)
    place_table = (
        place_index[None, :] == lax.broadcasted_iota(jnp.int32, (col_count * capacity, vesicles), 0)
    ).astype(jnp.float32)
    outgoing = jnp.dot(
        place_table, positions.reshape(vesicles, 2 * node_count), precision=highest
    ).reshape(col_count, capacity, 2, node_count)
    local_basis = old_basis.reshape(2, rank_count, source_count)
    local_sources = source_nodes.astype(jnp.float32)

    def owner_group(targets):
        kernel = far_kernel(targets, local_sources)
        return jnp.einsum(
            "eks,gedsn->gkdn", local_basis, kernel, preferred_element_type=jnp.float32
        )

    answers = lax.map(
        owner_group, lax.all_to_all(outgoing, "col", split_axis=0, concat_axis=0, tiled=True)
    )
    returned = lax.all_to_all(answers, "col", split_axis=0, concat_axis=0, tiled=True)
    sketch = jnp.dot(
        place_table.T,
        returned.reshape(col_count * capacity, rank_count * 2 * node_count),
        precision=highest,
    )
    sketch = sketch.reshape(vesicles, rank_count, 2 * node_count)
    local_gram = jnp.einsum("vkm,vjm->kj", sketch, sketch, precision=highest)
    gram = lax.psum(local_gram, ("clu", "col"))
    lower_factor = jnp.linalg.cholesky(gram)
    lower_inverse = jax.scipy.linalg.solve_triangular(
        lower_factor, jnp.eye(rank_count, dtype=jnp.float32), lower=True
    )
    scale_factor = math.sqrt(
        2.0 * node_count * vesicles * lax.axis_size("clu") * lax.axis_size("col")
    )
    new_basis = (
        jnp.einsum("kj,vjm->vkm", lower_inverse, sketch, precision=highest).reshape(
            vesicles, rank_count, 2, node_count
        )
        * scale_factor
    )
    return (force, near_velocity, new_basis)


def solution(mesh):
    placed = (
        P(("clu", "col"), None, None),
        P(("clu", "col"), None),
        P(("clu", "col")),
        P(("clu", "col"), None),
        P(("clu", "col"), None),
        P(("clu", "col")),
        P(("clu", "col"), None),
        P(None, "col"),
        P(None, "col"),
    )
    return jax.shard_map(
        per_device,
        mesh=mesh,
        in_specs=placed,
        out_specs=(
            P(("clu", "col"), None, None),
            P(("clu", "col"), None, None),
            P(("clu", "col"), None, None, None),
        ),
        check_vma=False,
    )
```

profile of v0, /device:TPU:1, one launch (start us, length us, event | category | flops | bytes accessed | tf_op | source)
XLA Modules:
  0.0 424.7 jit_solution(4086941855671178101)
XLA Ops:
  4.5 10.3 %all-to-all-start = ((f32[32,1,2]{2,1,0:T(1,128)}), f32[32,1,2]{2,1,0:T(1,128)S(1)}, u32[]{:S(2)}, u32[]{:S(2)}) async-start(f32[32,1,2]{2,1,0:T(1,128)} %bitcast.36), calls=%async_computation | async-start | bytes 32768 | tf_op jit(solution)/shard_map/all_to_all | solution.py:126
  21.8 13.1 %all-to-all-start.2 = ((f32[16,4,2,128]{3,2,1,0:T(2,128)}), f32[16,4,2,128]{3,2,1,0:T(2,128)S(1)}, u32[]{:S(2)}, u32[]{:S(2)}) async-start(f32[16,4,2,128]{3,2,1,0:T(2,128)} %copy.108), calls=%async_computation.2 | async-start | bytes 131072 | tf_op jit(solution)/shard_map/all_to_all | solution.py:177
  38.0 8.5 %all-to-all-done.2 = f32[16,4,2,128]{3,2,1,0:T(2,128)S(1)} async-done(((f32[16,4,2,128]{3,2,1,0:T(2,128)}), f32[16,4,2,128]{3,2,1,0:T(2,128)S(1)}, u32[]{:S(2)}, u32[]{:S(2)}) %all-to-all-start.2) | async-done | bytes 65568 | tf_op jit(solution)/shard_map/all_to_all | solution.py:177
  46.5 8.8 %all-to-all-start.1 = ((f32[32,2,4,128]{3,2,1,0:T(4,128)}), f32[32,2,4,128]{3,2,1,0:T(4,128)S(1)}, u32[]{:S(2)}, u32[]{:S(2)}) async-start(f32[32,2,4,128]{3,2,1,0:T(4,128)} %reshape.180), calls=%async_computation.1 | async-start | bytes 262144 | tf_op jit(solution)/shard_map/all_to_all | solution.py:125
  55.3 34.2 %while.21 = (s32[]{:T(128)}, f32[16,4,64,2,128]{4,2,3,1,0:T(8,128)}, f32[16,4,2,128]{3,2,1,0:T(2,128)S(1)}, f32[2,512]{1,0:T(2,128)S(1)}, bf16[2,64,512]{2,1,0:T(8,128)(2,1)S(1)}, /*index=5*/s32[]{:T(128)}) while((s32[]{:T(128)}, f32[16,4,64,2,128]{4,2,3,1,0:T(8,128)}, f32[16,4,2,128]{3,2,1,0:T(2,128)S(1)}, f32[2,512]{1,0:T(2,128)S(1)}, ...), condition=%wide.region_9.10_spmd, body=%wide.region_8.9_spmd.sunk | while | flops 143654912 | bytes 7774793 | solution.py:176
  58.4 1.2 fusion.155
  60.5 1.2 fusion.155
  62.7 1.2 fusion.155
  64.8 1.2 fusion.155
  67.0 1.2 fusion.155
  69.1 1.2 fusion.155
  71.2 1.2 fusion.155
  73.4 1.2 fusion.155
  75.5 1.2 fusion.155
  77.7 1.2 fusion.155
  79.8 1.2 fusion.155
  81.9 1.2 fusion.155
  84.1 1.2 fusion.155
  86.2 1.2 fusion.155
  88.3 1.2 fusion.155
  89.5 4.7 %all-to-all-start.3 = ((f32[16,4,64,2,128]{4,2,3,1,0:T(8,128)}), f32[16,4,64,2,128]{4,2,3,1,0:T(8,128)}, u32[]{:S(2)}, u32[]{:S(2)}) async-start(f32[16,4,64,2,128]{4,2,3,1,0:T(8,128)} %get-tuple-element.53), calls=%async_computation.3 | async-start | bytes 8388608 | tf_op jit(solution)/shard_map/all_to_all | solution.py:179
  94.2 8.9 %while.20 = (s32[]{:T(128)}, f32[16,4,2,128]{3,2,1,0:T(2,128)S(1)}, f32[16,4,2,128]{3,0,2,1:T(8,128)S(1)}, f32[16,4,4,128]{3,2,1,0:T(4,128)S(1)}, s32[]{:T(128)}) while((s32[]{:T(128)}, f32[16,4,2,128]{3,2,1,0:T(2,128)S(1)}, f32[16,4,2,128]{3,0,2,1:T(8,128)S(1)}, f32[16,4,4,128]{3,2,1,0:T(4,128)S(1)}, s32[]{:T(128)}) %tuple.83), condition=%wide.region_5.6_spmd, body=%wide.region_2.5_spmd.sunk | while | flops 1181698 | bytes 102473 | solution.py:143
  104.0 172.3 %all-to-all-done.3 = f32[16,4,64,2,128]{4,2,3,1,0:T(8,128)} async-done(((f32[16,4,64,2,128]{4,2,3,1,0:T(8,128)}), f32[16,4,64,2,128]{4,2,3,1,0:T(8,128)}, u32[]{:S(2)}, u32[]{:S(2)}) %all-to-all-start.3) | async-done | bytes 4194336 | tf_op jit(solution)/shard_map/all_to_all | solution.py:179
  276.3 8.0 %copy.110 = f32[16,4,64,2,128]{4,3,2,1,0:T(2,128)} copy(f32[16,4,64,2,128]{4,2,3,1,0:T(8,128)} %all-to-all-done.3) | data formatting | bytes 8388608 | tf_op jit(solution)/shard_map/all_to_all | solution.py:179
  284.3 6.4 %reshape.183 = f32[64,16384]{1,0:T(8,128)} reshape(f32[16,4,64,2,128]{4,3,2,1,0:T(2,128)} %copy.110) | data formatting | bytes 8388608 | tf_op jit(solution)/shard_map/reshape | solution.py:182
  290.7 3.8 fusion.36
  294.6 4.0 fusion.47
  298.6 105.8 %psum.7 = f32[64,64]{0,1:T(8,128)S(1)} all-reduce(f32[64,64]{0,1:T(8,128)S(1)} %fusion.47), channel_id=1, replica_groups=mesh['clu'=32,'col'=16] {'clu','col'}, use_global_device_ids=true, to_apply=%region_10.11 | all-reduce | flops 4096 | bytes 32768 | tf_op jit(solution)/shard_map/psum | solution.py:187
  404.5 5.8 %cholesky.17 = f32[64,64]{1,0:T(8,128)S(1)} custom-call(f32[64,64]{1,0:T(8,128)S(1)} %fusion.74), custom_call_target="Cholesky" | custom-call | tf_op jit(solution)/shard_map/jit(cholesky)/cholesky | solution.py:188
  411.7 4.9 %custom-call.7 = f32[1,64,64]{1,2,0:T(8,128)S(1)} custom-call(f32[1,64,64]{2,1,0:T(8,128)S(1)} %fusion.70), custom_call_target="InvertDiagBlocksLowerTriangular" | custom-call | tf_op jit(solution)/shard_map/jit(_solve_triangular)/triangular_solve | solution.py:189
  416.8 4.6 %multiply_bitcast_fusion = f32[32,64,256]{2,1,0:T(8,128)} fusion(f32[64,64,1]{1,0,2:T(8,128)S(1)} %convolution_bitcast_fusion, f32[32,64,256]{2,0,1:T(8,128)S(1)} %fusion.36), kind=kOutput, calls=%fused_computation.59 | convolution fusion | flops 403177472 | bytes 4210688 | tf_op jit(solution)/shard_map/kj,vjm->vkm/dot_general | solution.py:196
  421.4 3.2 mul.294
  (302 shorter events, 39.9 us)
Async XLA Ops:
  0.6 18.6 %copy-start = (f32[32,2,128]{2,1,0:T(2,128)S(1)}, f32[32,2,128]{2,1,0:T(2,128)}, u32[]{:S(2)}) copy-start(f32[32,2,128]{2,1,0:T(2,128)} %param.13) | copy-start | bytes 98308
  0.6 18.6 %copy-start.5 = (s32[1,32]{1,0:T(1,128)S(1)}, s32[1,32]{1,0:T(1,128)}, u32[]{:S(2)}) copy-start(s32[1,32]{1,0:T(1,128)} %param.16) | copy-start | bytes 388
  0.7 18.9 %copy-start.1 = (f32[32,128]{1,0:T(8,128)S(1)}, f32[32,128]{1,0:T(8,128)}, u32[]{:S(2)}) copy-start(f32[32,128]{1,0:T(8,128)} %param.14) | copy-start | bytes 49156
  0.7 19.1 %copy-start.3 = (f32[32]{0:T(128)S(1)}, f32[32]{0:T(128)}, u32[]{:S(2)}) copy-start(f32[32]{0:T(128)} %param.15) | copy-start | bytes 388
  0.7 34.9 %copy-start.2 = (bf16[2,512]{1,0:T(2,128)(2,1)S(1)}, bf16[2,512]{1,0:T(2,128)(2,1)}, u32[]{:S(2)}) copy-start(bf16[2,512]{1,0:T(2,128)(2,1)} %param.21) | copy-start | bytes 6148
  4.5 17.3 %all-to-all-start = ((f32[32,1,2]{2,1,0:T(1,128)}), f32[32,1,2]{2,1,0:T(1,128)S(1)}, u32[]{:S(2)}, u32[]{:S(2)}) async-start(f32[32,1,2]{2,1,0:T(1,128)} %bitcast.36), calls=%async_computation | async-start | bytes 32768 | tf_op jit(solution)/shard_map/all_to_all | solution.py:126
  17.2 38.2 %copy-start.4 = (bf16[128,512]{1,0:T(8,128)(2,1)S(1)}, bf16[128,512]{1,0:T(8,128)(2,1)}, u32[]{:S(2)}) copy-start(bf16[128,512]{1,0:T(8,128)(2,1)} %param.20) | copy-start | bytes 393220
  21.8 24.6 %all-to-all-start.2 = ((f32[16,4,2,128]{3,2,1,0:T(2,128)}), f32[16,4,2,128]{3,2,1,0:T(2,128)S(1)}, u32[]{:S(2)}, u32[]{:S(2)}) async-start(f32[16,4,2,128]{3,2,1,0:T(2,128)} %copy.108), calls=%async_computation.2 | async-start | bytes 131072 | tf_op jit(solution)/shard_map/all_to_all | solution.py:177
  46.5 43.0 %all-to-all-start.1 = ((f32[32,2,4,128]{3,2,1,0:T(4,128)}), f32[32,2,4,128]{3,2,1,0:T(4,128)S(1)}, u32[]{:S(2)}, u32[]{:S(2)}) async-start(f32[32,2,4,128]{3,2,1,0:T(4,128)} %reshape.180), calls=%async_computation.1 | async-start | bytes 262144 | tf_op jit(solution)/shard_map/all_to_all | solution.py:125
  89.5 186.7 %all-to-all-start.3 = ((f32[16,4,64,2,128]{4,2,3,1,0:T(8,128)}), f32[16,4,64,2,128]{4,2,3,1,0:T(8,128)}, u32[]{:S(2)}, u32[]{:S(2)}) async-start(f32[16,4,64,2,128]{4,2,3,1,0:T(8,128)} %get-tuple-element.53), calls=%async_computation.3 | async-start | bytes 8388608 | tf_op jit(solution)/shard_map/all_to_all | solution.py:179
where the time goes:
time: 425 us
  waiting for transfers between devices  181 us (43%)
  blocking collectives  106 us (25%)
  other arithmetic  38.8 us (9%)
  starting transfers between devices  36.9 us (9%)
  matrix products  36.4 us (9%)
  local copies, waits for them, and re-layouts  23 us (5%)
    all_to_all x1, waiting for transfers between devices, per_device(): lax.all_to_all(answers, 'col', split_axis=0, concat_axis=0, tiled=True)  172 us
    psum x1, blocking collectives, per_device(): gram = lax.psum(local_gram, ('clu', 'col'))  106 us
    dot_general x16, matrix products, owner_group(): jnp.einsum('eks,gedsn->gkdn', local_basis, kernel, preferred_element_type...  19.1 us
    all_to_all x1, starting transfers between devices, per_device(): lax.all_to_all(outgoing, 'col', split_axis=0, concat_axis=0, tiled=True)  13.1 us
    another operation x16, other arithmetic  12.1 us
    all_to_all x1, starting transfers between devices, per_device(): lax.all_to_all(target_tag, 'clu', split_axis=0, concat_axis=0, tiled=True)  10.3 us
    all_to_all x1, starting transfers between devices, per_device(): lax.all_to_all(packed, 'clu', split_axis=0, concat_axis=0, tiled=True)  8.83 us
  transfers between devices with their start and end apart: 4, of which 3 were waited for; matrix products, arithmetic and copies ran while one was open for 12% of the time, Pallas kernels for 0%

commit v1 on v0

v1 whole, which is shorter than its diff:
```python
import functools
import math

import jax
import jax.numpy as jnp
import numpy as np
from jax import lax
from jax.experimental import pallas as pl
from jax.experimental.pallas import tpu as pltpu
from jax.sharding import PartitionSpec as P

EPS_SQUARED = 0.01
HIGHEST = lax.Precision.HIGHEST
MESH = pl.DeviceIdType.MESH
SUB = 2


def spectral_tables(node_count):
    half_count = node_count // 2
    node_index = np.arange(node_count)[:, None]
    wave_index = np.arange(half_count + 1)[None, :]
    phase_angle = (node_index * wave_index % node_count) * (2.0 * math.pi / node_count)
    cosine_table = np.cos(phase_angle)
    sine_table = np.sin(phase_angle)
    wavenumber = np.arange(half_count + 1).astype(np.float64)
    inside = (wavenumber > 0) & (wavenumber < half_count)
    first_weight = np.where(inside, 2.0 * wavenumber / half_count, 0.0)
    fourth_weight = np.where(
        inside, 2.0 * (wavenumber / half_count) ** 4, np.where(wavenumber == half_count, 1.0, 0.0)
    )
    derivative = (
        (cosine_table * first_weight) @ sine_table.T - (sine_table * first_weight) @ cosine_table.T
    ) / node_count
    bending_table = (
        (cosine_table * fourth_weight) @ cosine_table.T
        + (sine_table * fourth_weight) @ sine_table.T
    ) / node_count
    return np.concatenate([derivative.T, bending_table.T], axis=1).astype(np.float32)


def iota(shape, dim):
    return lax.broadcasted_iota(jnp.int32, shape, dim)


def main_kernel(
    sizes,
    far_ref,
    table_ref,
    pos_ref,
    tension_ref,
    bending_ref,
    order_ref,
    dest_ref,
    goal_ref,
    basis_ref,
    nodes_ref,
    force_ref,
    near_ref,
    sketch_ref,
    gram_ref,
    move_out,
    move_in,
    goal_nodes,
    speeds,
    all_basis,
    all_nodes,
    kernels,
    sketch,
    part_out,
    part_in,
    ring_out,
    ring_in,
    sum_row,
    move_send,
    move_recv,
    node_send,
    node_recv,
    ring_send,
    ring_recv,
    pair_send,
    pair_recv,
    own_sem,
    part_send,
    part_recv,
    line_send,
    line_recv,
    full_send,
    full_recv,
    sketch_sem,
):
    n_clu, n_col, vesicles, node_count, move_count, rank_count, source_count = sizes
    me = lax.axis_index("clu")
    z = lax.axis_index("col")
    core = lax.rem(me, 2)
    partner = me + 1 - 2 * core
    up = {"col": lax.rem(z + 1, n_col)}
    down = {"col": lax.rem(z + n_col - 1, n_col)}
    plus_steps = n_col // 2
    minus_steps = n_col - 1 - plus_steps
    sub_rows = rank_count // SUB

    barrier = pltpu.get_barrier_semaphore()

    @pl.loop(1, n_clu)
    def _(k):
        pl.semaphore_signal(
            barrier, inc=1, device_id={"clu": lax.rem(me + k, n_clu)}, device_id_type=MESH
        )

    @pl.loop(1, n_col)
    def _(k):
        pl.semaphore_signal(
            barrier, inc=1, device_id={"col": lax.rem(z + k, n_col)}, device_id_type=MESH
        )

    pl.semaphore_wait(barrier, n_clu + n_col - 2)

    def node_copy(k):
        return pltpu.make_async_remote_copy(
            src_ref=nodes_ref,
            dst_ref=all_nodes.at[z],
            send_sem=node_send.at[k],
            recv_sem=node_recv.at[k],
            device_id={"col": lax.rem(z + k, n_col)},
            device_id_type=MESH,
        )

    @pl.loop(1, n_col)
    def _(k):
        node_copy(k).start()

    def ring_copy(way, step, sub):
        origin = lax.rem(z + n_col - step, n_col) if way == 0 else lax.rem(z + step, n_col)
        rows = pl.ds(sub * sub_rows, sub_rows)
        source = (
            basis_ref.at[core, rows] if step == 0 else all_basis.at[origin, core, rows]
        )
        return pltpu.make_async_remote_copy(
            src_ref=source,
            dst_ref=all_basis.at[origin, core, rows],
            send_sem=ring_send.at[way, step, sub],
            recv_sem=ring_recv.at[way, step, sub],
            device_id=up if way == 0 else down,
            device_id_type=MESH,
        )

    def ring_wait(way, step, sub):
        origin = (
            lax.rem(z + n_col - step - 1, n_col) if way == 0 else lax.rem(z + step + 1, n_col)
        )
        rows = pl.ds(sub * sub_rows, sub_rows)
        pltpu.make_async_remote_copy(
            src_ref=all_basis.at[origin, core, rows],
            dst_ref=all_basis.at[origin, core, rows],
            send_sem=ring_send.at[way, step, sub],
            recv_sem=ring_recv.at[way, step, sub],
            device_id=up if way == 0 else down,
            device_id_type=MESH,
        ).wait_recv()

    def pair_copy(offset, half):
        origin = lax.rem(z + offset, n_col)
        return pltpu.make_async_remote_copy(
            src_ref=all_basis.at[origin, half],
            dst_ref=all_basis.at[origin, half],
            send_sem=pair_send.at[offset],
            recv_sem=pair_recv.at[lax.rem(z + offset, n_col)],
            device_id={"clu": partner},
            device_id_type=MESH,
        )

    def ring_service(step):
        for way, count in ((0, plus_steps), (1, minus_steps)):
            if step < count:
                for sub in range(SUB):
                    ring_wait(way, step, sub)
                    if step + 1 < count:
                        ring_copy(way, step + 1, sub).start()
                offset = n_col - step - 1 if way == 0 else step + 1
                pair_copy(offset, core).start()

    for sub in range(SUB):
        ring_copy(0, 0, sub).start()
        ring_copy(1, 0, sub).start()
    own_basis = pltpu.make_async_copy(basis_ref, all_basis.at[z], own_sem.at[0])
    own_basis.start()
    own_nodes = pltpu.make_async_copy(nodes_ref, all_nodes.at[z], own_sem.at[1])
    own_nodes.start()

    rows_x = pl.ds(0, vesicles, stride=2)
    rows_y = pl.ds(1, vesicles, stride=2)
    flat = jnp.concatenate([pos_ref[rows_x, :], pos_ref[rows_y, :]], axis=0)
    table = table_ref[...]
    both = jnp.dot(flat, table, precision=HIGHEST, preferred_element_type=jnp.float32)
    slope = both[:, :node_count]
    fourth = both[:, node_count:]
    tension = tension_ref[...]
    pulled = slope * jnp.concatenate([tension, tension], axis=0)
    stretch = jnp.dot(
        pulled, table[:, :node_count], precision=HIGHEST, preferred_element_type=jnp.float32
    )
    square = (vesicles, vesicles)
    bending = jnp.sum(
        jnp.where(iota(square, 0) == iota(square, 1), bending_ref[...], 0.0), axis=1, keepdims=True
    )
    force = stretch - jnp.concatenate([bending, bending], axis=0) * fourth
    force_ref[rows_x, :] = force[:vesicles]
    force_ref[rows_y, :] = force[vesicles:]
    carried = jnp.concatenate([flat, force], axis=0)

    pairs = (move_count, move_count)
    dest_col = dest_ref[...].astype(jnp.float32)
    dest_row = jnp.sum(
        jnp.where(iota(pairs, 0) == iota(pairs, 1), dest_col, 0.0), axis=0, keepdims=True
    )
    earlier = jnp.sum(
        jnp.where((dest_col == dest_row) & (iota(pairs, 0) < iota(pairs, 1)), 1.0, 0.0),
        axis=0,
        keepdims=True,
    )
    slot_rows = n_clu * 8
    wide = (slot_rows, move_count)
    match = (dest_row == (iota(wide, 0) // 8).astype(jnp.float32)) & (
        earlier == (iota(wide, 0) // 4 % 2).astype(jnp.float32)
    )
    order_row = order_ref[:, :move_count].astype(jnp.float32)
    goal_row = goal_ref[...].astype(jnp.float32) + 1.0
    found = jnp.sum(jnp.where(match, 1.0, 0.0), axis=1, keepdims=True)
    chosen = jnp.sum(jnp.where(match, order_row, 0.0), axis=1, keepdims=True)
    goal = jnp.sum(jnp.where(match, goal_row, 0.0), axis=1, keepdims=True)
    table_shape = (slot_rows, 4 * vesicles)
    part_first = (iota(table_shape, 0) % 4 * vesicles).astype(jnp.float32)
    lane = iota(table_shape, 1).astype(jnp.float32)
    pack = jnp.where((lane == part_first + chosen) & (found > 0.0), 1.0, 0.0)
    packed = jnp.dot(pack, carried, precision=HIGHEST, preferred_element_type=jnp.float32)
    move_out[:, 0] = packed.reshape(n_clu, 8, node_count)
    move_out[:, 1] = jnp.broadcast_to(goal, (slot_rows, node_count)).reshape(n_clu, 8, node_count)

    def move_copy(k):
        other = lax.rem(me + k, n_clu)
        return pltpu.make_async_remote_copy(
            src_ref=move_out.at[other],
            dst_ref=move_in.at[me],
            send_sem=move_send.at[k],
            recv_sem=move_recv.at[k],
            device_id={"clu": other},
            device_id_type=MESH,
        )

    def from_peer(buffer, sems_out, sems_in, axis, k, count, index):
        other = lax.rem(index + count - k, count)
        return pltpu.make_async_remote_copy(
            src_ref=buffer.at[other],
            dst_ref=buffer.at[other],
            send_sem=sems_out.at[k],
            recv_sem=sems_in.at[k],
            device_id={axis: other},
            device_id_type=MESH,
        )

    @pl.loop(1, n_clu)
    def _(k):
        move_copy(k).start()

    own_move = pltpu.make_async_copy(move_out.at[me], move_in.at[me], own_sem.at[2])
    own_move.start()

    ring_service(0)
    own_nodes.wait()

    @pl.loop(1, n_col)
    def _(k):
        from_peer(all_nodes, node_send, node_recv, "col", k, n_col, z).wait_recv()

    chunk = 128

    def form_kernel(b):
        nodes = all_nodes[far_ref[b]]
        target_x = pos_ref[pl.ds(2 * b, 1), :]
        target_y = pos_ref[pl.ds(2 * b + 1, 1), :]
        for part in range(source_count // chunk):
            piece = nodes[:, part * chunk : (part + 1) * chunk]
            turned = jnp.concatenate([piece] * 4, axis=0).T
            delta_x = target_x - turned[:, 0:1]
            delta_y = target_y - turned[:, 1:2]
            square_x = delta_x * delta_x
            square_y = delta_y * delta_y
            spread = square_x + square_y + EPS_SQUARED
            log_part = -0.5 * jnp.log(spread)
            inverse = 1.0 / spread
            rows = pl.ds(part * chunk, chunk)
            kernels[b, rows, 0:node_count] = (log_part + square_x * inverse).astype(jnp.bfloat16)
            kernels[b, rows, node_count : 2 * node_count] = (
                delta_x * delta_y * inverse
            ).astype(jnp.bfloat16)
            kernels[b, rows, 2 * node_count : 3 * node_count] = (
                log_part + square_y * inverse
            ).astype(jnp.bfloat16)

    segments = max(plus_steps, 1)
    each = -(-vesicles // segments)
    for segment in range(segments):
        if segment > 0:
            ring_service(segment)

        @pl.loop(segment * each, min((segment + 1) * each, vesicles))
        def _(b):
            form_kernel(b)

    own_basis.wait()

    @pl.loop(1, n_col)
    def _(k):
        pair_copy(k, 1 - core).wait_recv()

    gram_shape = (2 * rank_count, 2 * rank_count)

    def sketch_row(b, total):
        basis = all_basis[far_ref[b]].reshape(2 * rank_count, source_count)
        product = jnp.dot(basis, kernels[b], preferred_element_type=jnp.float32)
        first = product[:rank_count]
        second = product[rank_count:]
        row = first[:, : 2 * node_count] + second[:, node_count:]
        sketch[b] = row
        high = row.astype(jnp.bfloat16)
        low = (row - high.astype(jnp.float32)).astype(jnp.bfloat16)
        stacked = jnp.concatenate([high, low], axis=0)
        return total + lax.dot_general(
            stacked, stacked, (((1,), (1,)), ((), ())), preferred_element_type=jnp.float32
        )

    total = lax.fori_loop(0, vesicles, sketch_row, jnp.zeros(gram_shape, jnp.float32))
    keep_sketch = pltpu.make_async_copy(sketch, sketch_ref, sketch_sem)
    keep_sketch.start()
    gram = (
        total[:rank_count, :rank_count]
        + total[:rank_count, rank_count:]
        + total[rank_count:, :rank_count]
        + total[rank_count:, rank_count:]
    )
    half = rank_count // 2
    folded = jnp.concatenate([gram[:half], gram[half:]], axis=1)
    own_rows = half // n_clu
    for row in range(half):
        part_out[row // own_rows, row % own_rows : row % own_rows + 1, :] = folded[row : row + 1]

    def part_copy(k):
        other = lax.rem(me + k, n_clu)
        return pltpu.make_async_remote_copy(
            src_ref=part_out.at[other],
            dst_ref=part_in.at[me],
            send_sem=part_send.at[k],
            recv_sem=part_recv.at[k],
            device_id={"clu": other},
            device_id_type=MESH,
        )

    @pl.loop(1, n_clu)
    def _(k):
        part_copy(k).start()

    own_move.wait()

    @pl.loop(1, n_clu)
    def _(k):
        from_peer(move_in, move_send, move_recv, "clu", k, n_clu, me).wait_recv()

    goals = move_in[:, 1].reshape(slot_rows, node_count)
    goal_shape = (slot_rows, 2 * vesicles)
    part_index = iota(goal_shape, 0) % 4
    goal_lane = iota(goal_shape, 1).astype(jnp.float32)
    goal_value = goals[:, : 2 * vesicles]
    goal_hot = jnp.where(
        (goal_lane == (part_index * vesicles - 1).astype(jnp.float32) + goal_value)
        & (part_index < 2)
        & (goal_value > 0.0),
        1.0,
        0.0,
    )
    goal_nodes[...] = jnp.dot(
        goal_hot, flat, precision=HIGHEST, preferred_element_type=jnp.float32
    ).reshape(n_clu, 8, node_count)

    def near_pair(src):
        turned = move_in[src, 0].T
        goal_tile = goal_nodes[src]
        results = []
        for slot in range(2):
            first = 4 * slot
            delta_x = goal_tile[first : first + 1] - turned[:, first : first + 1]
            delta_y = goal_tile[first + 1 : first + 2] - turned[:, first + 1 : first + 2]
            push_x = turned[:, first + 2 : first + 3]
            push_y = turned[:, first + 3 : first + 4]
            spread = delta_x * delta_x + delta_y * delta_y + EPS_SQUARED
            log_part = -0.5 * jnp.log(spread)
            along = (delta_x * push_x + delta_y * push_y) / spread
            results.append(jnp.sum(log_part * push_x + delta_x * along, axis=0, keepdims=True))
            results.append(jnp.sum(log_part * push_y + delta_y * along, axis=0, keepdims=True))
            results.append(jnp.zeros((2, node_count), jnp.float32))
        speeds[src] = jnp.concatenate(results, axis=0)

    @pl.loop(0, n_clu // 2)
    def _(src):
        near_pair(src)

    part_in[me] = part_out[me]

    @pl.loop(1, n_clu)
    def _(k):
        from_peer(part_in, part_send, part_recv, "clu", k, n_clu, me).wait_recv()

    ring_out[...] = jnp.sum(part_in[...], axis=0)

    def line_copy(k):
        return pltpu.make_async_remote_copy(
            src_ref=ring_out,
            dst_ref=ring_in.at[z],
            send_sem=line_send.at[k],
            recv_sem=line_recv.at[k],
            device_id={"col": lax.rem(z + k, n_col)},
            device_id_type=MESH,
        )

    @pl.loop(1, n_col)
    def _(k):
        line_copy(k).start()

    @pl.loop(n_clu // 2, n_clu)
    def _(src):
        near_pair(src)

    ring_in[z] = ring_out[...]

    @pl.loop(1, n_col)
    def _(k):
        from_peer(ring_in, line_send, line_recv, "col", k, n_col, z).wait_recv()

    sum_row[...] = jnp.sum(ring_in[...], axis=0)

    def full_copy(k):
        return pltpu.make_async_remote_copy(
            src_ref=sum_row,
            dst_ref=gram_ref.at[me],
            send_sem=full_send.at[k],
            recv_sem=full_recv.at[k],
            device_id={"clu": lax.rem(me + k, n_clu)},
            device_id_type=MESH,
        )

    @pl.loop(1, n_clu)
    def _(k):
        full_copy(k).start()

    gram_ref[me] = sum_row[...]
    near = lax.dot_general(
        goal_hot,
        speeds[...].reshape(slot_rows, node_count),
        (((0,), (0,)), ((), ())),
        precision=HIGHEST,
        preferred_element_type=jnp.float32,
    ) * (1.0 / node_count)
    near_ref[rows_x, :] = near[:vesicles]
    near_ref[rows_y, :] = near[vesicles:]

    for step in range(plus_steps):
        for way, count in ((0, plus_steps), (1, minus_steps)):
            if step < count:
                for sub in range(SUB):
                    ring_copy(way, step, sub).wait_send()

    @pl.loop(1, n_col)
    def _(k):
        node_copy(k).wait_send()
        line_copy(k).wait_send()
        pair_copy(k, core).wait_send()

    keep_sketch.wait()

    @pl.loop(1, n_clu)
    def _(k):
        move_copy(k).wait_send()
        part_copy(k).wait_send()
        full_copy(k).wait_send()
        from_peer(gram_ref, full_send, full_recv, "clu", k, n_clu, me).wait_recv()


def finish_kernel(
    scale_factor, gram_ref, sketch_ref, force_in, near_in, basis_out, force_out, near_out, inverse
):
    rank_count = sketch_ref.shape[1]
    node_count = sketch_ref.shape[2] // 2

    @pl.when(pl.program_id(0) == 0)
    def _():
        force_out[...] = force_in[...]
        near_out[...] = near_in[...]
        folded = gram_ref[...]
        gram = jnp.concatenate([folded[:, :rank_count], folded[:, rank_count:]], axis=0)
        square = (rank_count, rank_count)
        eye = jnp.where(iota(square, 0) == iota(square, 1), 1.0, 0.0)
        joined = jnp.concatenate([gram, eye], axis=1)
        tiles = [joined[8 * t : 8 * t + 8] for t in range(rank_count // 8)]
        below = iota((8, 1), 0)
        for j in range(rank_count):
            home, spot = divmod(j, 8)
            pivot_row = tiles[home][spot : spot + 1]
            scaled = pivot_row / pivot_row[:, j : j + 1]
            for t in range(home, rank_count // 8):
                factor = tiles[t][:, j : j + 1]
                if t == home:
                    factor = jnp.where(below > spot, factor, 0.0)
                tiles[t] = tiles[t] - factor * scaled
        whole = jnp.concatenate(tiles, axis=0)
        pivots = jnp.sum(whole[:, :rank_count] * eye, axis=1, keepdims=True)
        inverse[...] = whole[:, rank_count:] * (scale_factor / jnp.sqrt(pivots))

    lower = inverse[...]
    for b in range(sketch_ref.shape[0]):
        result = jnp.dot(
            lower, sketch_ref[b], precision=HIGHEST, preferred_element_type=jnp.float32
        )
        basis_out[b, pl.ds(0, rank_count, stride=2), :] = result[:, :node_count]
        basis_out[b, pl.ds(1, rank_count, stride=2), :] = result[:, node_count:]


def per_device(
    positions,
    tension,
    bending,
    moved_order,
    move_destination,
    move_target,
    far_range,
    old_basis,
    source_nodes,
):
    n_clu, n_col = lax.axis_size("clu"), lax.axis_size("col")
    vesicles, node_count = positions.shape[0], positions.shape[2]
    move_count = move_target.shape[0]
    rank_count, source_count = old_basis.shape[0] // 2, old_basis.shape[1]
    half = rank_count // 2
    own_rows = half // n_clu
    plus_steps = n_col // 2
    f32, bf16 = jnp.float32, jnp.bfloat16
    vmem, dma = pltpu.VMEM, pltpu.SemaphoreType.DMA
    in_vmem = pl.BlockSpec(memory_space=pltpu.VMEM)
    sizes = (n_clu, n_col, vesicles, node_count, move_count, rank_count, source_count)
    force, near, sketch, gram = pl.pallas_call(
        functools.partial(main_kernel, sizes),
        out_shape=(
            jax.ShapeDtypeStruct((2 * vesicles, node_count), f32),
            jax.ShapeDtypeStruct((2 * vesicles, node_count), f32),
            jax.ShapeDtypeStruct((vesicles, rank_count, 2 * node_count), f32),
            jax.ShapeDtypeStruct((n_clu, own_rows, 2 * rank_count), f32),
        ),
        in_specs=[pl.BlockSpec(memory_space=pltpu.SMEM)] + [in_vmem] * 9,
        out_specs=(in_vmem, in_vmem, pl.BlockSpec(memory_space=pl.ANY), in_vmem),
        scratch_shapes=[
            vmem((n_clu, 2, 8, node_count), f32),
            vmem((n_clu, 2, 8, node_count), f32),
            vmem((n_clu, 8, node_count), f32),
            vmem((n_clu, 8, node_count), f32),
            vmem((n_col, 2, rank_count, source_count), bf16),
            vmem((n_col, 2, source_count), f32),
            vmem((vesicles, source_count, 3 * node_count), bf16),
            vmem((vesicles, rank_count, 2 * node_count), f32),
            vmem((n_clu, own_rows, 2 * rank_count), f32),
            vmem((n_clu, own_rows, 2 * rank_count), f32),
            vmem((own_rows, 2 * rank_count), f32),
            vmem((n_col, own_rows, 2 * rank_count), f32),
            vmem((own_rows, 2 * rank_count), f32),
            dma((n_clu,)),
            dma((n_clu,)),
            dma((n_col,)),
            dma((n_col,)),
            dma((2, plus_steps, SUB)),
            dma((2, plus_steps, SUB)),
            dma((n_col,)),
            dma((n_col,)),
            dma((3,)),
            dma((n_clu,)),
            dma((n_clu,)),
            dma((n_col,)),
            dma((n_col,)),
            dma((n_clu,)),
            dma((n_clu,)),
            dma,
        ],
        compiler_params=pltpu.CompilerParams(
            collective_id=0, has_side_effects=True, vmem_limit_bytes=48 * 1024 * 1024
        ),
        name="main_step",
    )(
        far_range.reshape(vesicles),
        jnp.asarray(spectral_tables(node_count)),
        positions.reshape(2 * vesicles, node_count),
        tension,
        bending.reshape(1, vesicles),
        moved_order,
        move_destination,
        move_target.reshape(1, move_count),
        old_basis.reshape(2, rank_count, source_count),
        source_nodes.astype(f32),
    )
    scale_factor = math.sqrt(2.0 * node_count * vesicles * n_clu * n_col)
    group = 4
    flat_spec = pl.BlockSpec((2 * vesicles, node_count), lambda i: (0, 0))
    new_basis, force, near = pl.pallas_call(
        functools.partial(finish_kernel, scale_factor),
        out_shape=(
            jax.ShapeDtypeStruct((vesicles, 2 * rank_count, node_count), f32),
            jax.ShapeDtypeStruct((2 * vesicles, node_count), f32),
            jax.ShapeDtypeStruct((2 * vesicles, node_count), f32),
        ),
        grid=(vesicles // group,),
        in_specs=[
            pl.BlockSpec((half, 2 * rank_count), lambda i: (0, 0)),
            pl.BlockSpec((group, rank_count, 2 * node_count), lambda i: (i, 0, 0)),
            flat_spec,
            flat_spec,
        ],
        out_specs=(
            pl.BlockSpec((group, 2 * rank_count, node_count), lambda i: (i, 0, 0)),
            flat_spec,
            flat_spec,
        ),
        scratch_shapes=[vmem((rank_count, rank_count), f32)],
        name="finish_step",
    )(gram.reshape(half, 2 * rank_count), sketch, force, near)
    return (
        force.reshape(vesicles, 2, node_count),
        near.reshape(vesicles, 2, node_count),
        new_basis.reshape(vesicles, rank_count, 2, node_count),
    )


def solution(mesh):
    placed = (
        P(("clu", "col"), None, None),
        P(("clu", "col"), None),
        P(("clu", "col")),
        P(("clu", "col"), None),
        P(("clu", "col"), None),
        P(("clu", "col")),
        P(("clu", "col"), None),
        P(None, "col"),
        P(None, "col"),
    )
    return jax.shard_map(
        per_device,
        mesh=mesh,
        in_specs=placed,
        out_specs=(
            P(("clu", "col"), None, None),
            P(("clu", "col"), None, None),
            P(("clu", "col"), None, None, None),
        ),
        check_vma=False,
    )
```

time: 425 us -> 110 us (0.26)
  waiting for transfers between devices: 181 us -> 0 us
  blocking collectives: 106 us -> 0 us
  Pallas kernels: 0 us -> 98.1 us
  other arithmetic: 38.8 us -> 0.69 us
  starting transfers between devices: 36.9 us -> 0 us
  matrix products: 36.4 us -> 0 us
  local copies, waits for them, and re-layouts: 23 us -> 9.76 us
    all_to_all x4 -> x0, waiting for transfers between devices: 181 us -> none  [the longest x1 172 us: per_device(): lax.all_to_all(answers, 'col', split_axis=0, concat_axis=0, tiled=True)]
    psum x1 -> x0, blocking collectives: 106 us -> none  [per_device(): gram = lax.psum(local_gram, ('clu', 'col'))]
    pallas_call x0 -> x2, Pallas kernels: none -> 98.1 us  [the longest x1 85.6 us: per_device(): pl.pallas_call(functools.partial(main_kernel, sizes), out_shape=(jax.Shap...]
    all_to_all x4 -> x0, starting transfers between devices: 36.9 us -> none  [the longest x1 13.1 us: per_device(): lax.all_to_all(outgoing, 'col', split_axis=0, concat_axis=0, tiled=True)]
    dot_general x32 -> x0, matrix products: 36.2 us -> none  [the longest x16 19.1 us: owner_group(): jnp.einsum('eks,gedsn->gkdn', local_basis, kernel, preferred_element_type...]
    another operation x39 -> x0, other arithmetic: 26.7 us -> none
    all_to_all x3 -> x0, local copies, waits for them, and re-layouts: 9.29 us -> none  [the longest x1 8.03 us: per_device(): lax.all_to_all(answers, 'col', split_axis=0, concat_axis=0, tiled=True)]
    unnamed x15 -> x25, local copies, waits for them, and re-layouts: 1.32 us -> 9.76 us
  transfers between devices with their start and end apart: 4 -> 0, of which waited for: 3 -> 0; matrix products, arithmetic and copies ran while one was open for 12% -> 0% of each run, Pallas kernels for 0% -> 0%
where the time goes in v1:
time: 110 us; the launch traced here: 109 us
  Pallas kernels  98.1 us (89%)
  local copies, waits for them, and re-layouts  9.76 us (9%)
    pallas_call x1, Pallas kernels, per_device(): pl.pallas_call(functools.partial(main_kernel, sizes), out_shape=(jax.Shap...  85.6 us
    pallas_call x1, Pallas kernels, per_device(): pl.pallas_call(functools.partial(finish_kernel, scale_factor), out_shape=...  12.5 us
    unnamed x25, local copies, waits for them, and re-layouts  9.76 us

profile of v1, /device:TPU:1, one launch (start us, length us, event | category | flops | bytes accessed | tf_op | source)
XLA Modules:
  0.0 109.2 jit_solution(7557542336670940759)
XLA Ops:
  0.6 0.7 convert_element_type.3.nodes_ref
  1.3 0.7 copy.13.dest_ref
  2.0 0.0 copy-start.1
  2.1 0.9 copy-done.1
  3.0 0.0 copy-start.2
  3.0 0.9 copy-done.2
  3.9 0.0 copy-start.5
  3.9 0.8 copy-done.5
  4.6 0.0 copy-start.7
  4.6 0.7 copy-done.7
  5.3 0.0 copy-start.8
  5.3 0.7 copy-done.8
  6.0 0.0 copy-start.9
  6.0 0.7 copy-done.9
  6.6 0.0 copy-start.10
  6.6 0.7 copy-done.10
  7.3 0.0 copy-start.11
  7.3 0.7 copy-done.11
  8.0 85.6 %main_step.1 = (f32[64,128]{1,0:T(8,128)S(1)}, f32[64,128]{1,0:T(8,128)S(1)}, f32[32,64,256]{2,1,0:T(8,128)S(1)}, f32[32,1,128]{2,1,0:T(1,128)S(1)}) custom-call(s32[32]{0:T(128)S(1)} %bitcast.12, f32[128,256]{1,0:T(8,128)S(1)} %copy-done.2, f32[64,128]{1,0:T(8,128)S(1)} %bitcast.10, f32[32,128]{1,0:T(8,128)S(1)} %copy-done.7, f32[1,32]{1,0:T(1,128)S(1)} %bitcast.13, ...), custom_call_target="tpu_custom_call" | custom-call | tf_op jit(solution)/shard_map/main_step/pallas_call | solution.py:548
  93.6 0.0 copy-start
  93.6 1.3 %copy-done = f32[32,64,256]{2,1,0:T(8,128)} copy-done((f32[32,64,256]{2,1,0:T(8,128)}, f32[32,64,256]{2,1,0:T(8,128)S(1)}, u32[]{:S(2)}) %copy-start) | copy-done | bytes 2097176
  94.9 0.0 copy-start.3
  94.9 0.6 copy-done.3
  95.5 0.0 copy-start.4
  95.5 0.6 copy-done.4
  96.1 0.0 copy-start.6
  96.1 0.6 copy-done.6
  96.7 12.5 %finish_step.1 = (f32[32,128,128]{2,1,0:T(8,128)}, f32[64,128]{1,0:T(8,128)}, f32[64,128]{1,0:T(8,128)}) custom-call(f32[32,128]{1,0:T(8,128)} %bitcast.11, f32[32,64,256]{2,1,0:T(8,128)} %copy-done, f32[64,128]{1,0:T(8,128)} %copy-done.3, f32[64,128]{1,0:T(8,128)} %copy-done.4), custom_call_target="tpu_custom_call" | custom-call | tf_op jit(solution)/shard_map/finish_step/pallas_call | solution.py:608
Async XLA Ops:
  2.0 0.9 copy-start.1
  3.0 0.9 copy-start.2
  3.9 0.8 copy-start.5
  4.6 0.7 copy-start.7
  5.3 0.7 copy-start.8
  6.0 0.7 copy-start.9
  6.6 0.7 copy-start.10
  7.3 0.7 copy-start.11
  93.6 1.3 %copy-start = (f32[32,64,256]{2,1,0:T(8,128)}, f32[32,64,256]{2,1,0:T(8,128)S(1)}, u32[]{:S(2)}) copy-start(f32[32,64,256]{2,1,0:T(8,128)S(1)} %get-tuple-element.11.sketch_ref) | copy-start | bytes 6291460
  94.9 0.6 copy-start.3
  95.5 0.6 copy-start.4
  96.1 0.6 copy-start.6

commit v2 on v1

v2 whole, which is shorter than its diff:
```python
import functools
import math

import jax
import jax.numpy as jnp
import numpy as np
from jax import lax
from jax.experimental import pallas as pl
from jax.experimental.pallas import tpu as pltpu
from jax.sharding import PartitionSpec as P

EPS_SQUARED = 0.01
HIGHEST = lax.Precision.HIGHEST
MESH = pl.DeviceIdType.MESH
SUB = 4
ROWS = 8
VMEM_ALL = 67043328


def spectral_tables(node_count):
    half_count = node_count // 2
    node_index = np.arange(node_count)[:, None]
    wave_index = np.arange(half_count + 1)[None, :]
    phase_angle = (node_index * wave_index % node_count) * (2.0 * math.pi / node_count)
    cosine_table = np.cos(phase_angle)
    sine_table = np.sin(phase_angle)
    wavenumber = np.arange(half_count + 1).astype(np.float64)
    inside = (wavenumber > 0) & (wavenumber < half_count)
    first_weight = np.where(inside, 2.0 * wavenumber / half_count, 0.0)
    fourth_weight = np.where(
        inside, 2.0 * (wavenumber / half_count) ** 4, np.where(wavenumber == half_count, 1.0, 0.0)
    )
    derivative = (
        (cosine_table * first_weight) @ sine_table.T - (sine_table * first_weight) @ cosine_table.T
    ) / node_count
    bending_table = (
        (cosine_table * fourth_weight) @ cosine_table.T
        + (sine_table * fourth_weight) @ sine_table.T
    ) / node_count
    return np.concatenate([derivative.T, bending_table.T], axis=1).astype(np.float32)


def iota(shape, dim):
    return lax.broadcasted_iota(jnp.int32, shape, dim)


def main_kernel(
    sizes,
    far_hbm,
    table_hbm,
    pos_hbm,
    tension_hbm,
    bending_hbm,
    order_hbm,
    dest_hbm,
    goal_hbm,
    basis_ref,
    nodes_ref,
    force_out,
    near_out,
    split_out,
    gram_out,
    force_ref,
    near_ref,
    split_ref,
    gram_ref,
    far_ref,
    table_ref,
    pos_ref,
    tension_ref,
    bending_ref,
    order_ref,
    dest_ref,
    goal_ref,
    move_out,
    move_in,
    goal_nodes,
    speeds,
    all_basis,
    all_nodes,
    wide_nodes,
    kernels,
    part_out,
    part_in,
    line_out,
    line_in,
    sum_row,
    move_send,
    move_recv,
    node_send,
    node_recv,
    ring_send,
    ring_recv,
    pair_send,
    pair_recv,
    own_sem,
    part_send,
    part_recv,
    line_send,
    line_recv,
    full_send,
    full_recv,
):
    n_clu, n_col, vesicles, node_count, move_count, rank_count, source_count = sizes
    me = lax.axis_index("clu")
    z = lax.axis_index("col")
    core = lax.rem(me, 2)
    partner = me + 1 - 2 * core
    up = {"col": lax.rem(z + 1, n_col)}
    down = {"col": lax.rem(z + n_col - 1, n_col)}
    plus_steps = n_col // 2
    minus_steps = n_col - 1 - plus_steps
    sub_rows = rank_count // SUB

    barrier = pltpu.get_barrier_semaphore()

    @pl.loop(1, n_col)
    def _(k):
        pl.semaphore_signal(
            barrier, inc=1, device_id={"col": lax.rem(z + k, n_col)}, device_id_type=MESH
        )

    @pl.loop(1, n_clu)
    def _(k):
        pl.semaphore_signal(
            barrier, inc=1, device_id={"clu": lax.rem(me + k, n_clu)}, device_id_type=MESH
        )

    loads = [
        pltpu.make_async_copy(source, place, own_sem.at[3 + at])
        for at, (source, place) in enumerate(
            (
                (pos_hbm, pos_ref),
                (table_hbm, table_ref),
                (tension_hbm, tension_ref),
                (bending_hbm, bending_ref),
                (order_hbm, order_ref),
                (dest_hbm, dest_ref),
                (goal_hbm, goal_ref),
                (far_hbm, far_ref),
            )
        )
    ]
    for load in loads:
        load.start()
    keeps = [
        pltpu.make_async_copy(source, place, own_sem.at[11 + at])
        for at, (source, place) in enumerate(
            (
                (force_ref, force_out),
                (near_ref, near_out),
                (split_ref, split_out),
                (gram_ref, gram_out),
            )
        )
    ]
    own_basis = pltpu.make_async_copy(basis_ref, all_basis.at[z], own_sem.at[0])
    own_basis.start()
    own_nodes = pltpu.make_async_copy(nodes_ref, all_nodes.at[z], own_sem.at[1])
    own_nodes.start()
    for load in loads:
        load.wait()

    rows_x = pl.ds(0, vesicles, stride=2)
    rows_y = pl.ds(1, vesicles, stride=2)
    flat = jnp.concatenate([pos_ref[rows_x, :], pos_ref[rows_y, :]], axis=0)
    table = table_ref[...]
    both = jnp.dot(flat, table, precision=HIGHEST, preferred_element_type=jnp.float32)
    slope = both[:, :node_count]
    fourth = both[:, node_count:]
    tension = tension_ref[...]
    pulled = slope * jnp.concatenate([tension, tension], axis=0)
    stretch = jnp.dot(
        pulled, table[:, :node_count], precision=HIGHEST, preferred_element_type=jnp.float32
    )
    square = (vesicles, vesicles)
    bending = jnp.sum(
        jnp.where(iota(square, 0) == iota(square, 1), bending_ref[...], 0.0), axis=1, keepdims=True
    )
    force = stretch - jnp.concatenate([bending, bending], axis=0) * fourth
    force_ref[rows_x, :] = force[:vesicles]
    force_ref[rows_y, :] = force[vesicles:]
    keeps[0].start()
    carried = jnp.concatenate([flat, force], axis=0)

    pairs = (move_count, move_count)
    dest_row = dest_ref[...].astype(jnp.float32)
    dest_col = jnp.sum(
        jnp.where(iota(pairs, 0) == iota(pairs, 1), dest_row, 0.0), axis=1, keepdims=True
    )
    earlier = jnp.sum(
        jnp.where((dest_col == dest_row) & (iota(pairs, 0) < iota(pairs, 1)), 1.0, 0.0),
        axis=0,
        keepdims=True,
    )
    slot_rows = n_clu * 8
    wide = (slot_rows, move_count)
    match = (dest_row == (iota(wide, 0) // 8).astype(jnp.float32)) & (
        earlier == (iota(wide, 0) // 4 % 2).astype(jnp.float32)
    )
    order_row = order_ref[:, :move_count].astype(jnp.float32)
    goal_row = goal_ref[...].astype(jnp.float32) + 1.0
    found = jnp.sum(jnp.where(match, 1.0, 0.0), axis=1, keepdims=True)
    chosen = jnp.sum(jnp.where(match, order_row, 0.0), axis=1, keepdims=True)
    goal = jnp.sum(jnp.where(match, goal_row, 0.0), axis=1, keepdims=True)
    table_shape = (slot_rows, 4 * vesicles)
    part_first = (iota(table_shape, 0) % 4 * vesicles).astype(jnp.float32)
    lane = iota(table_shape, 1).astype(jnp.float32)
    pack = jnp.where((lane == part_first + chosen) & (found > 0.0), 1.0, 0.0)
    packed = jnp.dot(pack, carried, precision=HIGHEST, preferred_element_type=jnp.float32)
    move_out[:, 0] = packed.reshape(n_clu, 8, node_count)
    move_out[:, 1] = jnp.broadcast_to(goal, (slot_rows, node_count)).reshape(n_clu, 8, node_count)

    def node_copy(k):
        return pltpu.make_async_remote_copy(
            src_ref=nodes_ref,
            dst_ref=all_nodes.at[z],
            send_sem=node_send.at[k],
            recv_sem=node_recv.at[k],
            device_id={"col": lax.rem(z + k, n_col)},
            device_id_type=MESH,
        )

    def ring_copy(way, step, sub, source):
        origin = lax.rem(z + n_col - step, n_col) if way == 0 else lax.rem(z + step, n_col)
        rows = pl.ds(pl.multiple_of(sub * sub_rows, sub_rows), sub_rows)
        return pltpu.make_async_remote_copy(
            src_ref=all_basis.at[origin, core, rows] if source is None else source.at[core, rows],
            dst_ref=all_basis.at[origin, core, rows],
            send_sem=ring_send.at[way, step, sub],
            recv_sem=ring_recv.at[way, step, sub],
            device_id=up if way == 0 else down,
            device_id_type=MESH,
        )

    def pair_copy(offset, half):
        origin = lax.rem(z + offset, n_col)
        return pltpu.make_async_remote_copy(
            src_ref=all_basis.at[origin, half],
            dst_ref=all_basis.at[origin, half],
            send_sem=pair_send.at[offset],
            recv_sem=pair_recv.at[offset],
            device_id={"clu": partner},
            device_id_type=MESH,
        )

    def service(index):
        step, sub = lax.div(index, SUB), lax.rem(index, SUB)
        for way, count in ((0, plus_steps), (1, minus_steps)):

            @pl.when(step < count)
            def _():
                origin = (
                    lax.rem(z + n_col - step - 1, n_col)
                    if way == 0
                    else lax.rem(z + step + 1, n_col)
                )
                rows = pl.ds(pl.multiple_of(sub * sub_rows, sub_rows), sub_rows)
                pltpu.make_async_remote_copy(
                    src_ref=all_basis.at[origin, core, rows],
                    dst_ref=all_basis.at[origin, core, rows],
                    send_sem=ring_send.at[way, step, sub],
                    recv_sem=ring_recv.at[way, step, sub],
                    device_id=up if way == 0 else down,
                    device_id_type=MESH,
                ).wait_recv()

                @pl.when(step + 1 < count)
                def _():
                    ring_copy(way, step + 1, sub, None).start()

                @pl.when(sub == SUB - 1)
                def _():
                    pair_copy(n_col - step - 1 if way == 0 else step + 1, core).start()

    def move_copy(k):
        other = lax.rem(me + k, n_clu)
        return pltpu.make_async_remote_copy(
            src_ref=move_out.at[other],
            dst_ref=move_in.at[me],
            send_sem=move_send.at[k],
            recv_sem=move_recv.at[k],
            device_id={"clu": other},
            device_id_type=MESH,
        )

    def from_peer(buffer, sems_out, sems_in, axis, k, count, index):
        other = lax.rem(index + count - k, count)
        return pltpu.make_async_remote_copy(
            src_ref=buffer.at[other],
            dst_ref=buffer.at[other],
            send_sem=sems_out.at[k],
            recv_sem=sems_in.at[k],
            device_id={axis: other},
            device_id_type=MESH,
        )

    pl.semaphore_wait(barrier, n_clu + n_col - 2)

    @pl.loop(1, n_col)
    def _(k):
        node_copy(k).start()

    for sub in range(SUB):
        ring_copy(0, 0, sub, basis_ref).start()
        ring_copy(1, 0, sub, basis_ref).start()

    @pl.loop(1, n_clu)
    def _(k):
        move_copy(k).start()

    own_move = pltpu.make_async_copy(move_out.at[me], move_in.at[me], own_sem.at[2])
    own_move.start()

    services = plus_steps * SUB
    early = services // 4

    @pl.loop(0, early)
    def _(index):
        service(index)

    own_nodes.wait()

    @pl.loop(1, n_col)
    def _(k):
        from_peer(all_nodes, node_send, node_recv, "col", k, n_col, z).wait_recv()

    chunk = 128
    parts = source_count // chunk
    for quarter in range(4):
        for origin in range(quarter * n_col // 4, (quarter + 1) * n_col // 4):
            for part in range(parts):
                piece = all_nodes[origin, :, part * chunk : (part + 1) * chunk].astype(jnp.float32)
                turned = jnp.concatenate([piece] * 4, axis=0).T
                rows = pl.ds(part * chunk, chunk)
                wide_nodes[origin, rows, :node_count] = jnp.broadcast_to(
                    turned[:, 0:1], (chunk, node_count)
                )
                wide_nodes[origin, rows, node_count:] = jnp.broadcast_to(
                    turned[:, 1:2], (chunk, node_count)
                )
        service(early + quarter)

    def form_kernel(b):
        own = far_ref[0, b]
        target_x = pos_ref[pl.ds(2 * b, 1), :]
        target_y = pos_ref[pl.ds(2 * b + 1, 1), :]
        for part in range(parts):
            rows = slice(part * chunk, (part + 1) * chunk)
            delta_x = target_x - wide_nodes[own, rows, :node_count]
            delta_y = target_y - wide_nodes[own, rows, node_count:]
            square_x = delta_x * delta_x
            square_y = delta_y * delta_y
            spread = square_x + square_y + EPS_SQUARED
            log_part = -0.5 * jnp.log(spread)
            inverse = 1.0 / spread
            kernels[b, rows, 0:node_count] = (log_part + square_x * inverse).astype(jnp.bfloat16)
            kernels[b, rows, node_count : 2 * node_count] = (
                delta_x * delta_y * inverse
            ).astype(jnp.bfloat16)
            kernels[b, rows, 2 * node_count : 3 * node_count] = (
                log_part + square_y * inverse
            ).astype(jnp.bfloat16)

    begun = early + 4
    rounds = vesicles // 2
    within = min(rounds, services - begun)

    @pl.loop(0, rounds)
    def _(turn):
        @pl.when(turn < within)
        def _():
            service(begun + turn)

        form_kernel(2 * turn)
        form_kernel(2 * turn + 1)

    @pl.loop(begun + within, services)
    def _(index):
        service(index)

    own_basis.wait()

    @pl.loop(1, n_col)
    def _(k):
        pair_copy(k, 1 - core).wait_recv()

    width = 2 * node_count

    def sketch_row(b):
        basis = all_basis[far_ref[0, b]].reshape(2 * rank_count, source_count)
        product = jnp.dot(basis, kernels[b], preferred_element_type=jnp.float32)
        row = product[:rank_count, :width] + product[rank_count:, node_count:]
        high = row.astype(jnp.bfloat16)
        lanes = pl.ds(pl.multiple_of(b * width, width), width)
        split_ref[:rank_count, lanes] = high
        split_ref[rank_count:, lanes] = (row - high.astype(jnp.float32)).astype(jnp.bfloat16)

    @pl.loop(0, vesicles // ROWS)
    def _(turn):
        for at in range(ROWS):
            sketch_row(turn * ROWS + at)

    keeps[2].start()
    split = split_ref[...]
    total = lax.dot_general(
        split, split, (((1,), (1,)), ((), ())), preferred_element_type=jnp.float32
    )
    gram = (
        total[:rank_count, :rank_count]
        + total[:rank_count, rank_count:]
        + total[rank_count:, :rank_count]
        + total[rank_count:, rank_count:]
    )
    half = rank_count // 2
    folded = jnp.concatenate([gram[:half], gram[half:]], axis=1)
    own_rows = half // n_clu
    for row in range(half):
        part_out[row // own_rows, row % own_rows : row % own_rows + 1, :] = folded[row : row + 1]

    def part_copy(k):
        other = lax.rem(me + k, n_clu)
        return pltpu.make_async_remote_copy(
            src_ref=part_out.at[other],
            dst_ref=part_in.at[me],
            send_sem=part_send.at[k],
            recv_sem=part_recv.at[k],
            device_id={"clu": other},
            device_id_type=MESH,
        )

    @pl.loop(1, n_clu)
    def _(k):
        part_copy(k).start()

    own_move.wait()

    @pl.loop(1, n_clu)
    def _(k):
        from_peer(move_in, move_send, move_recv, "clu", k, n_clu, me).wait_recv()

    goals = move_in[:, 1].reshape(slot_rows, node_count)
    goal_shape = (slot_rows, 2 * vesicles)
    part_index = iota(goal_shape, 0) % 4
    goal_lane = iota(goal_shape, 1).astype(jnp.float32)
    goal_value = goals[:, : 2 * vesicles]
    goal_hot = jnp.where(
        (goal_lane == (part_index * vesicles - 1).astype(jnp.float32) + goal_value)
        & (part_index < 2)
        & (goal_value > 0.0),
        1.0,
        0.0,
    )
    goal_nodes[...] = jnp.dot(
        goal_hot, flat, precision=HIGHEST, preferred_element_type=jnp.float32
    ).reshape(n_clu, 8, node_count)

    def near_pair(src):
        turned = move_in[src, 0].T
        goal_tile = goal_nodes[src]
        results = []
        for slot in range(2):
            first = 4 * slot
            delta_x = goal_tile[first : first + 1] - turned[:, first : first + 1]
            delta_y = goal_tile[first + 1 : first + 2] - turned[:, first + 1 : first + 2]
            push_x = turned[:, first + 2 : first + 3]
            push_y = turned[:, first + 3 : first + 4]
            spread = delta_x * delta_x + delta_y * delta_y + EPS_SQUARED
            log_part = -0.5 * jnp.log(spread)
            along = (delta_x * push_x + delta_y * push_y) * (1.0 / spread)
            results.append(jnp.sum(log_part * push_x + delta_x * along, axis=0, keepdims=True))
            results.append(jnp.sum(log_part * push_y + delta_y * along, axis=0, keepdims=True))
            results.append(jnp.zeros((2, node_count), jnp.float32))
        speeds[src] = jnp.concatenate(results, axis=0)

    @pl.loop(0, n_clu // 4)
    def _(turn):
        near_pair(2 * turn)
        near_pair(2 * turn + 1)

    part_in[me] = part_out[me]

    @pl.loop(1, n_clu)
    def _(k):
        from_peer(part_in, part_send, part_recv, "clu", k, n_clu, me).wait_recv()

    line_out[...] = jnp.sum(part_in[...], axis=0)

    def line_copy(k):
        return pltpu.make_async_remote_copy(
            src_ref=line_out,
            dst_ref=line_in.at[z],
            send_sem=line_send.at[k],
            recv_sem=line_recv.at[k],
            device_id={"col": lax.rem(z + k, n_col)},
            device_id_type=MESH,
        )

    @pl.loop(1, n_col)
    def _(k):
        line_copy(k).start()

    @pl.loop(n_clu // 4, n_clu // 2)
    def _(turn):
        near_pair(2 * turn)
        near_pair(2 * turn + 1)

    near = lax.dot_general(
        goal_hot,
        speeds[...].reshape(slot_rows, node_count),
        (((0,), (0,)), ((), ())),
        precision=HIGHEST,
        preferred_element_type=jnp.float32,
    ) * (1.0 / node_count)
    near_ref[rows_x, :] = near[:vesicles]
    near_ref[rows_y, :] = near[vesicles:]
    keeps[1].start()
    line_in[z] = line_out[...]

    @pl.loop(1, n_col)
    def _(k):
        from_peer(line_in, line_send, line_recv, "col", k, n_col, z).wait_recv()

    sum_row[...] = jnp.sum(line_in[...], axis=0)

    def full_copy(k):
        return pltpu.make_async_remote_copy(
            src_ref=sum_row,
            dst_ref=gram_ref.at[me],
            send_sem=full_send.at[k],
            recv_sem=full_recv.at[k],
            device_id={"clu": lax.rem(me + k, n_clu)},
            device_id_type=MESH,
        )

    @pl.loop(1, n_clu)
    def _(k):
        full_copy(k).start()

    gram_ref[me] = sum_row[...]

    @pl.loop(0, services)
    def _(index):
        step, sub = lax.div(index, SUB), lax.rem(index, SUB)
        ring_copy(0, step, sub, None).wait_send()

        @pl.when(step < minus_steps)
        def _():
            ring_copy(1, step, sub, None).wait_send()

    @pl.loop(1, n_col)
    def _(k):
        node_copy(k).wait_send()
        line_copy(k).wait_send()
        pair_copy(k, core).wait_send()

    @pl.loop(1, n_clu)
    def _(k):
        move_copy(k).wait_send()
        part_copy(k).wait_send()

    @pl.loop(1, n_clu)
    def _(k):
        full_copy(k).wait_send()
        from_peer(gram_ref, full_send, full_recv, "clu", k, n_clu, me).wait_recv()

    keeps[3].start()
    for keep in keeps:
        keep.wait()


def lower_inverse(gram):
    rank_count = gram.shape[0]
    square = (rank_count, rank_count)
    eye = jnp.where(iota(square, 0) == iota(square, 1), 1.0, 0.0)
    joined = jnp.concatenate([gram, eye], axis=1)
    width = 2 * rank_count
    count = rank_count // 8
    tiles = [joined[8 * t : 8 * t + 8] for t in range(count)]
    row_of = iota((8, width), 0)
    for first in range(0, rank_count, 4):
        home, spot = divmod(first, 8)
        tile = tiles[home]
        rows = [tile[spot + i : spot + i + 1] for i in range(4)]
        pivot = [
            [
                jnp.broadcast_to(rows[i][:, first + k : first + k + 1], (1, width))
                for k in range(4)
            ]
            for i in range(4)
        ]
        columns = {
            t: [
                jnp.broadcast_to(tiles[t][:, first + k : first + k + 1], (8, width))
                for k in range(4)
            ]
            for t in range(home, count)
        }
        inverses = []
        for i in range(4):
            inverses.append(1.0 / pivot[i][i])
            for m in range(i + 1, 4):
                ratio = pivot[i][m] * inverses[i]
                rows[m] = rows[m] - ratio * rows[i]
                for k in range(m, 4):
                    pivot[m][k] = pivot[m][k] - ratio * pivot[i][k]
        for t in range(home, count):
            factors = []
            for i in range(4):
                value = columns[t][i]
                for q in range(i):
                    value = value - factors[q] * pivot[q][i]
                factors.append(value * inverses[i])
            updated = tiles[t] - (
                (factors[0] * rows[0] + factors[1] * rows[1])
                + (factors[2] * rows[2] + factors[3] * rows[3])
            )
            if t == home:
                updated = jnp.where(row_of > spot + 3, updated, tile)
                for i in range(1, 4):
                    updated = jnp.where(row_of == spot + i, rows[i], updated)
            tiles[t] = updated
    whole = jnp.concatenate(tiles, axis=0)
    pivots = jnp.sum(whole[:, :rank_count] * eye, axis=1, keepdims=True)
    return whole[:, rank_count:] / jnp.sqrt(pivots)


def finish_kernel(
    scale_factor,
    gram_in,
    split_in,
    force_in,
    near_in,
    basis_out,
    force_out,
    near_out,
    gram_ref,
    split_ref,
    force_ref,
    near_ref,
    spread_ref,
    staged,
    sems,
):
    vesicles, rows, node_count = staged.shape
    rank_count = rows // 2
    loads = [
        pltpu.make_async_copy(source, place, sems.at[2 + at])
        for at, (source, place) in enumerate(
            (
                (gram_in, gram_ref),
                (force_in, force_ref),
                (near_in, near_ref),
                (split_in, split_ref),
            )
        )
    ]
    for load in loads:
        load.start()
    loads[0].wait()
    folded = gram_ref[...]
    gram = jnp.concatenate([folded[:, :rank_count], folded[:, rank_count:]], axis=0)
    lower = lower_inverse(gram) * scale_factor
    for load in loads[1:]:
        load.wait()
    send_force = pltpu.make_async_copy(force_ref, force_out, sems.at[0])
    send_near = pltpu.make_async_copy(near_ref, near_out, sems.at[1])
    send_force.start()
    send_near.start()
    zeros = jnp.zeros_like(lower)
    spread_ref[pl.ds(0, rank_count, stride=2), :] = jnp.concatenate([lower, zeros], axis=1)
    spread_ref[pl.ds(1, rank_count, stride=2), :] = jnp.concatenate([zeros, lower], axis=1)
    spread = spread_ref[...]
    high = spread.astype(jnp.bfloat16)
    low = (spread - high.astype(jnp.float32)).astype(jnp.bfloat16)
    factors = jnp.concatenate([high, low, high, low], axis=1)
    group = 4
    sends = []
    for first in range(0, vesicles, group):
        for b in range(first, first + group):
            lanes = slice(2 * b * node_count, (2 * b + 1) * node_count)
            others = slice((2 * b + 1) * node_count, (2 * b + 2) * node_count)
            upper = [split_ref[:rank_count, lanes], split_ref[:rank_count, others]]
            under = [split_ref[rank_count:, lanes], split_ref[rank_count:, others]]
            staged[b] = jnp.dot(
                factors,
                jnp.concatenate(upper + upper + under + under, axis=0),
                preferred_element_type=jnp.float32,
            )
        rows_now = pl.ds(first, group)
        send = pltpu.make_async_copy(
            staged.at[rows_now], basis_out.at[rows_now], sems.at[6 + first // group]
        )
        send.start()
        sends.append(send)
    for send in sends:
        send.wait()
    send_force.wait()
    send_near.wait()


def per_device(
    positions,
    tension,
    bending,
    moved_order,
    move_destination,
    move_target,
    far_range,
    old_basis,
    source_nodes,
):
    n_clu, n_col = lax.axis_size("clu"), lax.axis_size("col")
    vesicles, node_count = positions.shape[0], positions.shape[2]
    move_count = move_target.shape[0]
    rank_count, source_count = old_basis.shape[0] // 2, old_basis.shape[1]
    half = rank_count // 2
    own_rows = half // n_clu
    plus_steps = n_col // 2
    f32, bf16, i32 = jnp.float32, jnp.bfloat16, jnp.int32
    vmem, dma = pltpu.VMEM, pltpu.SemaphoreType.DMA
    in_hbm = pl.BlockSpec(memory_space=pltpu.HBM)
    sizes = (n_clu, n_col, vesicles, node_count, move_count, rank_count, source_count)
    flat_shape = jax.ShapeDtypeStruct((2 * vesicles, node_count), f32)
    force, near, split, gram = pl.pallas_call(
        functools.partial(main_kernel, sizes),
        out_shape=(
            flat_shape,
            flat_shape,
            jax.ShapeDtypeStruct((2 * rank_count, vesicles * 2 * node_count), bf16),
            jax.ShapeDtypeStruct((n_clu, own_rows, 2 * rank_count), f32),
        ),
        in_specs=[in_hbm] * 10,
        out_specs=[in_hbm] * 4,
        scratch_shapes=[
            vmem((2 * vesicles, node_count), f32),
            vmem((2 * vesicles, node_count), f32),
            vmem((2 * rank_count, vesicles * 2 * node_count), bf16),
            vmem((n_clu, own_rows, 2 * rank_count), f32),
            pltpu.SMEM((1, vesicles), i32),
            vmem((node_count, 2 * node_count), f32),
            vmem((2 * vesicles, node_count), f32),
            vmem((vesicles, node_count), f32),
            vmem((1, vesicles), f32),
            vmem((1, vesicles), i32),
            vmem((1, move_count), i32),
            vmem((1, move_count), i32),
            vmem((n_clu, 2, 8, node_count), f32),
            vmem((n_clu, 2, 8, node_count), f32),
            vmem((n_clu, 8, node_count), f32),
            vmem((n_clu, 8, node_count), f32),
            vmem((n_col, 2, rank_count, source_count), bf16),
            vmem((n_col, 2, source_count), bf16),
            vmem((n_col, source_count, 2 * node_count), f32),
            vmem((vesicles, source_count, 3 * node_count), bf16),
            vmem((n_clu, own_rows, 2 * rank_count), f32),
            vmem((n_clu, own_rows, 2 * rank_count), f32),
            vmem((own_rows, 2 * rank_count), f32),
            vmem((n_col, own_rows, 2 * rank_count), f32),
            vmem((own_rows, 2 * rank_count), f32),
            dma((n_clu,)),
            dma((n_clu,)),
            dma((n_col,)),
            dma((n_col,)),
            dma((2, plus_steps, SUB)),
            dma((2, plus_steps, SUB)),
            dma((n_col,)),
            dma((n_col,)),
            dma((15,)),
            dma((n_clu,)),
            dma((n_clu,)),
            dma((n_col,)),
            dma((n_col,)),
            dma((n_clu,)),
            dma((n_clu,)),
        ],
        compiler_params=pltpu.CompilerParams(
            collective_id=0, has_side_effects=True, vmem_limit_bytes=VMEM_ALL
        ),
        name="main_step",
    )(
        far_range.reshape(1, vesicles),
        jnp.asarray(spectral_tables(node_count)),
        positions.reshape(2 * vesicles, node_count),
        tension,
        bending.reshape(1, vesicles),
        moved_order,
        move_destination.reshape(1, move_count),
        move_target.reshape(1, move_count),
        old_basis.reshape(2, rank_count, source_count),
        source_nodes,
    )
    scale_factor = math.sqrt(2.0 * node_count * vesicles * n_clu * n_col)
    new_basis, force, near = pl.pallas_call(
        functools.partial(finish_kernel, scale_factor),
        out_shape=(
            jax.ShapeDtypeStruct((vesicles, 2 * rank_count, node_count), f32),
            flat_shape,
            flat_shape,
        ),
        in_specs=[in_hbm] * 4,
        out_specs=[in_hbm] * 3,
        scratch_shapes=[
            vmem((half, 2 * rank_count), f32),
            vmem((2 * rank_count, vesicles * 2 * node_count), bf16),
            vmem((2 * vesicles, node_count), f32),
            vmem((2 * vesicles, node_count), f32),
            vmem((2 * rank_count, 2 * rank_count), f32),
            vmem((vesicles, 2 * rank_count, node_count), f32),
            dma((6 + vesicles // 4,)),
        ],
        compiler_params=pltpu.CompilerParams(vmem_limit_bytes=VMEM_ALL),
        name="finish_step",
    )(gram.reshape(half, 2 * rank_count), split, force, near)
    return (
        force.reshape(vesicles, 2, node_count),
        near.reshape(vesicles, 2, node_count),
        new_basis.reshape(vesicles, rank_count, 2, node_count),
    )


def solution(mesh):
    placed = (
        P(("clu", "col"), None, None),
        P(("clu", "col"), None),
        P(("clu", "col")),
        P(("clu", "col"), None),
        P(("clu", "col"), None),
        P(("clu", "col")),
        P(("clu", "col"), None),
        P(None, "col"),
        P(None, "col"),
    )
    return jax.shard_map(
        per_device,
        mesh=mesh,
        in_specs=placed,
        out_specs=(
            P(("clu", "col"), None, None),
            P(("clu", "col"), None, None),
            P(("clu", "col"), None, None, None),
        ),
        check_vma=False,
    )
```

time: 110 us -> 77.9 us (0.71)
  Pallas kernels: 98.1 us -> 77 us
  local copies, waits for them, and re-layouts: 9.76 us -> 0 us
    pallas_call x1, Pallas kernels: 85.6 us -> 72 us  [per_device(): pl.pallas_call(functools.partial(main_kernel, sizes), out_shape=(flat_sha...]
    unnamed x25 -> x0, local copies, waits for them, and re-layouts: 9.76 us -> none
    pallas_call x1, Pallas kernels: 12.5 us -> 5.08 us  [per_device(): pl.pallas_call(functools.partial(finish_kernel, scale_factor), out_shape=...]
where the time goes in v2:
time: 77.9 us; the launch traced here: 77.7 us
  Pallas kernels  77 us (99%)
    pallas_call x1, Pallas kernels, per_device(): pl.pallas_call(functools.partial(main_kernel, sizes), out_shape=(flat_sha...  72 us
    pallas_call x1, Pallas kernels, per_device(): pl.pallas_call(functools.partial(finish_kernel, scale_factor), out_shape=...  5.08 us

profile of v2, /device:TPU:1, one launch (start us, length us, event | category | flops | bytes accessed | tf_op | source)
XLA Modules:
  0.0 77.7 jit_solution(7705352200831071978)
XLA Ops:
  0.6 72.0 %main_step.1 = (f32[64,128]{1,0:T(8,128)}, f32[64,128]{1,0:T(8,128)}, bf16[128,8192]{1,0:T(8,128)(2,1)}, f32[32,1,128]{2,1,0:T(1,128)}) custom-call(s32[1,32]{1,0:T(1,128)} %bitcast.13, f32[128,256]{1,0:T(8,128)} %constant.2.clone.table_hbm, f32[64,128]{1,0:T(8,128)} %bitcast.11, f32[32,128]{1,0:T(8,128)} %tension_hbm.1, f32[1,32]{1,0:T(1,128)} %bitcast.14, ...), custom_call_target="tpu_custom_call" | custom-call | tf_op jit(solution)/shard_map/main_step/pallas_call | solution.py:725
  72.6 5.1 %finish_step.1 = (f32[32,128,128]{2,1,0:T(8,128)}, f32[64,128]{1,0:T(8,128)}, f32[64,128]{1,0:T(8,128)}) custom-call(f32[32,128]{1,0:T(8,128)} %bitcast.12, bf16[128,8192]{1,0:T(8,128)(2,1)} %get-tuple-element.11.split_in, f32[64,128]{1,0:T(8,128)} %get-tuple-element.12.force_in, f32[64,128]{1,0:T(8,128)} %get-tuple-element.13.near_in), custom_call_target="tpu_custom_call" | custom-call | tf_op jit(solution)/shard_map/finish_step/pallas_call | solution.py:794

commit v3 on v2

--- a/solution.py
+++ b/solution.py
@@ -12,7 +12,10 @@
 EPS_SQUARED = 0.01
 HIGHEST = lax.Precision.HIGHEST
 MESH = pl.DeviceIdType.MESH
-SUB = 4
+CHIPS_X = 4
+LAG = 6
+MOVE_TURN = 12
+DELAY = 4
 ROWS = 8
 VMEM_ALL = 67043328
 
@@ -55,7 +58,7 @@
     dest_hbm,
     goal_hbm,
     basis_ref,
-    nodes_ref,
+    nodes_hbm,
     force_out,
     near_out,
     split_out,
@@ -91,6 +94,10 @@
     node_recv,
     ring_send,
     ring_recv,
+    first_send,
+    first_recv,
+    second_send,
+    second_recv,
     pair_send,
     pair_recv,
     own_sem,
@@ -106,11 +113,13 @@
     z = lax.axis_index("col")
     core = lax.rem(me, 2)
     partner = me + 1 - 2 * core
-    up = {"col": lax.rem(z + 1, n_col)}
-    down = {"col": lax.rem(z + n_col - 1, n_col)}
-    plus_steps = n_col // 2
-    minus_steps = n_col - 1 - plus_steps
-    sub_rows = rank_count // SUB
+    chips = min(CHIPS_X, n_clu // 2)
+    members = 2 * chips
+    plane = lax.div(me, members)
+    across = lax.div(lax.rem(me, members), 2)
+    major = across + core * (plane - across)
+    minor = plane + core * (across - plane)
+    lane_share = source_count // chips
 
     barrier = pltpu.get_barrier_semaphore()
 
@@ -156,8 +165,9 @@
     ]
     own_basis = pltpu.make_async_copy(basis_ref, all_basis.at[z], own_sem.at[0])
     own_basis.start()
-    own_nodes = pltpu.make_async_copy(nodes_ref, all_nodes.at[z], own_sem.at[1])
-    own_nodes.start()
+    load_nodes = pltpu.make_async_copy(nodes_hbm, all_nodes.at[z], own_sem.at[1])
+    load_nodes.start()
+    load_nodes.wait()
     for load in loads:
         load.wait()
 
@@ -213,7 +223,7 @@
 
     def node_copy(k):
         return pltpu.make_async_remote_copy(
-            src_ref=nodes_ref,
+            src_ref=nodes_hbm,
             dst_ref=all_nodes.at[z],
             send_sem=node_send.at[k],
             recv_sem=node_recv.at[k],
@@ -221,57 +231,104 @@
             device_id_type=MESH,
         )
 
-    def ring_copy(way, step, sub, source):
-        origin = lax.rem(z + n_col - step, n_col) if way == 0 else lax.rem(z + step, n_col)
-        rows = pl.ds(pl.multiple_of(sub * sub_rows, sub_rows), sub_rows)
-        return pltpu.make_async_remote_copy(
-            src_ref=all_basis.at[origin, core, rows] if source is None else source.at[core, rows],
-            dst_ref=all_basis.at[origin, core, rows],
-            send_sem=ring_send.at[way, step, sub],
-            recv_sem=ring_recv.at[way, step, sub],
-            device_id=up if way == 0 else down,
-            device_id_type=MESH,
-        )
-
-    def pair_copy(offset, half):
-        origin = lax.rem(z + offset, n_col)
-        return pltpu.make_async_remote_copy(
-            src_ref=all_basis.at[origin, half],
-            dst_ref=all_basis.at[origin, half],
-            send_sem=pair_send.at[offset],
-            recv_sem=pair_recv.at[offset],
+    def line_offset(turn):
+        odd = lax.rem(turn, 2)
+        return (1 - odd) * (lax.div(turn, 2) + 1) + odd * (n_col - lax.div(turn + 1, 2))
+
+    def peer(down, right):
+        first = lax.rem(minor + down, chips)
+        second = lax.rem(major + right, chips)
+        return {
+            "clu": (first + core * (second - first)) * members
+            + 2 * (second + core * (first - second))
+            + core
+        }
+
+    def tile(ref, row, column):
+        lanes = pl.ds(pl.multiple_of(column * lane_share, lane_share), lane_share)
+        return ref.at[core, row, :, lanes]
+
+    def origin_of(k):
+        return lax.rem(z + n_col - k, n_col)
+
+    def ring_copy(k):
+        return pltpu.make_async_remote_copy(
+            src_ref=tile(basis_ref, major, minor),
+            dst_ref=tile(all_basis.at[z], major, minor),
+            send_sem=ring_send.at[k],
+            recv_sem=ring_recv.at[k],
+            device_id={"col": lax.rem(z + k, n_col)},
+            device_id_type=MESH,
+        )
+
+    def from_ring(k):
+        block = tile(all_basis.at[origin_of(k)], major, minor)
+        return pltpu.make_async_remote_copy(
+            src_ref=block,
+            dst_ref=block,
+            send_sem=ring_send.at[k],
+            recv_sem=ring_recv.at[k],
+            device_id={"col": origin_of(k)},
+            device_id_type=MESH,
+        )
+
+    def first_copy(k, d, back):
+        column = lax.rem(minor + back * (chips - d), chips)
+        block = tile(all_basis.at[origin_of(k)], major, column)
+        return pltpu.make_async_remote_copy(
+            src_ref=block,
+            dst_ref=block,
+            send_sem=first_send.at[k, d],
+            recv_sem=first_recv.at[k, d],
+            device_id=peer(chips - d if back else d, 0),
+            device_id_type=MESH,
+        )
+
+    def second_copy(k, d, back):
+        row = lax.rem(major + back * (chips - d), chips)
+        block = all_basis.at[origin_of(k), core, row]
+        return pltpu.make_async_remote_copy(
+            src_ref=block,
+            dst_ref=block,
+            send_sem=second_send.at[k, d],
+            recv_sem=second_recv.at[k, d],
+            device_id=peer(0, chips - d if back else d),
+            device_id_type=MESH,
+        )
+
+    def pair_copy(k, half):
+        block = all_basis.at[origin_of(k), half]
+        return pltpu.make_async_remote_copy(
+            src_ref=block,
+            dst_ref=block,
+            send_sem=pair_send.at[k],
+            recv_sem=pair_recv.at[k],
             device_id={"clu": partner},
             device_id_type=MESH,
         )
 
-    def service(index):
-        step, sub = lax.div(index, SUB), lax.rem(index, SUB)
-        for way, count in ((0, plus_steps), (1, minus_steps)):
-
-            @pl.when(step < count)
-            def _():
-                origin = (
-                    lax.rem(z + n_col - step - 1, n_col)
-                    if way == 0
-                    else lax.rem(z + step + 1, n_col)
-                )
-                rows = pl.ds(pl.multiple_of(sub * sub_rows, sub_rows), sub_rows)
-                pltpu.make_async_remote_copy(
-                    src_ref=all_basis.at[origin, core, rows],
-                    dst_ref=all_basis.at[origin, core, rows],
-                    send_sem=ring_send.at[way, step, sub],
-                    recv_sem=ring_recv.at[way, step, sub],
-                    device_id=up if way == 0 else down,
-                    device_id_type=MESH,
-                ).wait_recv()
-
-                @pl.when(step + 1 < count)
-                def _():
-                    ring_copy(way, step + 1, sub, None).start()
-
-                @pl.when(sub == SUB - 1)
-                def _():
-                    pair_copy(n_col - step - 1 if way == 0 else step + 1, core).start()
+    def service(turn):
+        @pl.when(turn < n_col - 1)
+        def _():
+            k = line_offset(turn)
+            from_ring(k).wait_recv()
+            for d in range(1, chips):
+                first_copy(k, d, 0).start()
+
+        @pl.when((turn >= LAG) & (turn < n_col - 1 + LAG))
+        def _():
+            k = line_offset(turn - LAG)
+            for d in range(1, chips):
+                first_copy(k, d, 1).wait_recv()
+            for d in range(1, chips):
+                second_copy(k, d, 0).start()
+
+        @pl.when(turn >= 2 * LAG)
+        def _():
+            k = line_offset(turn - 2 * LAG)
+            for d in range(1, chips):
+                second_copy(k, d, 1).wait_recv()
+            pair_copy(k, core).start()
 
     def move_copy(k):
         other = lax.rem(me + k, n_clu)
@@ -301,45 +358,39 @@
     def _(k):
         node_copy(k).start()
 
-    for sub in range(SUB):
-        ring_copy(0, 0, sub, basis_ref).start()
-        ring_copy(1, 0, sub, basis_ref).start()
-
-    @pl.loop(1, n_clu)
-    def _(k):
-        move_copy(k).start()
-
-    own_move = pltpu.make_async_copy(move_out.at[me], move_in.at[me], own_sem.at[2])
-    own_move.start()
-
-    services = plus_steps * SUB
-    early = services // 4
-
-    @pl.loop(0, early)
-    def _(index):
-        service(index)
-
-    own_nodes.wait()
-
-    @pl.loop(1, n_col)
-    def _(k):
-        from_peer(all_nodes, node_send, node_recv, "col", k, n_col, z).wait_recv()
-
+    @pl.loop(0, n_col - 1)
+    def _(turn):
+        ring_copy(line_offset(turn)).start()
+
+    services = n_col - 1 + 2 * LAG
+    early = n_col - 1 - DELAY
     chunk = 128
     parts = source_count // chunk
-    for quarter in range(4):
-        for origin in range(quarter * n_col // 4, (quarter + 1) * n_col // 4):
-            for part in range(parts):
-                piece = all_nodes[origin, :, part * chunk : (part + 1) * chunk].astype(jnp.float32)
-                turned = jnp.concatenate([piece] * 4, axis=0).T
-                rows = pl.ds(part * chunk, chunk)
-                wide_nodes[origin, rows, :node_count] = jnp.broadcast_to(
-                    turned[:, 0:1], (chunk, node_count)
-                )
-                wide_nodes[origin, rows, node_count:] = jnp.broadcast_to(
-                    turned[:, 1:2], (chunk, node_count)
-                )
-        service(early + quarter)
+
+    def widen(origin):
+        nodes = all_nodes[origin].astype(jnp.float32)
+        for part in range(parts):
+            piece = nodes[:, part * chunk : (part + 1) * chunk]
+            turned = jnp.concatenate([piece] * 4, axis=0).T
+            rows = slice(part * chunk, (part + 1) * chunk)
+            wide_nodes[origin, rows, :node_count] = jnp.broadcast_to(
+                turned[:, 0:1], (chunk, node_count)
+            )
+            wide_nodes[origin, rows, node_count:] = jnp.broadcast_to(
+                turned[:, 1:2], (chunk, node_count)
+            )
+
+    widen(z)
+
+    @pl.loop(0, n_col - 1)
+    def _(turn):
+        k = line_offset(turn)
+        from_peer(all_nodes, node_send, node_recv, "col", k, n_col, z).wait_recv()
+        widen(origin_of(k))
+
+        @pl.when(turn >= DELAY)
+        def _():
+            service(turn - DELAY)
 
     def form_kernel(b):
         own = far_ref[0, b]
@@ -362,18 +413,26 @@
                 log_part + square_y * inverse
             ).astype(jnp.bfloat16)
 
-    begun = early + 4
+    own_move = pltpu.make_async_copy(move_out.at[me], move_in.at[me], own_sem.at[2])
+    own_move.start()
+    begun = early
     rounds = vesicles // 2
     within = min(rounds, services - begun)
 
     @pl.loop(0, rounds)
     def _(turn):
+        form_kernel(2 * turn)
+        form_kernel(2 * turn + 1)
+
         @pl.when(turn < within)
         def _():
             service(begun + turn)
 
-        form_kernel(2 * turn)
-        form_kernel(2 * turn + 1)
+        @pl.when(turn == min(MOVE_TURN, rounds - 1))
+        def _():
+            @pl.loop(1, n_clu)
+            def _(k):
+                move_copy(k).start()
 
     @pl.loop(begun + within, services)
     def _(index):
@@ -539,20 +598,15 @@
 
     gram_ref[me] = sum_row[...]
 
-    @pl.loop(0, services)
-    def _(index):
-        step, sub = lax.div(index, SUB), lax.rem(index, SUB)
-        ring_copy(0, step, sub, None).wait_send()
-
-        @pl.when(step < minus_steps)
-        def _():
-            ring_copy(1, step, sub, None).wait_send()
-
     @pl.loop(1, n_col)
     def _(k):
         node_copy(k).wait_send()
         line_copy(k).wait_send()
         pair_copy(k, core).wait_send()
+        ring_copy(k).wait_send()
+        for d in range(1, chips):
+            first_copy(k, d, 0).wait_send()
+            second_copy(k, d, 0).wait_send()
 
     @pl.loop(1, n_clu)
     def _(k):
@@ -716,7 +770,8 @@
     rank_count, source_count = old_basis.shape[0] // 2, old_basis.shape[1]
     half = rank_count // 2
     own_rows = half // n_clu
-    plus_steps = n_col // 2
+    chips = min(CHIPS_X, n_clu // 2)
+    row_share = rank_count // chips
     f32, bf16, i32 = jnp.float32, jnp.bfloat16, jnp.int32
     vmem, dma = pltpu.VMEM, pltpu.SemaphoreType.DMA
     in_hbm = pl.BlockSpec(memory_space=pltpu.HBM)
@@ -749,7 +804,7 @@
             vmem((n_clu, 2, 8, node_count), f32),
             vmem((n_clu, 8, node_count), f32),
             vmem((n_clu, 8, node_count), f32),
-            vmem((n_col, 2, rank_count, source_count), bf16),
+            vmem((n_col, 2, chips, row_share, source_count), bf16),
             vmem((n_col, 2, source_count), bf16),
             vmem((n_col, source_count, 2 * node_count), f32),
             vmem((vesicles, source_count, 3 * node_count), bf16),
@@ -762,8 +817,12 @@
             dma((n_clu,)),
             dma((n_col,)),
             dma((n_col,)),
-            dma((2, plus_steps, SUB)),
-            dma((2, plus_steps, SUB)),
+            dma((n_col,)),
+            dma((n_col,)),
+            dma((n_col, chips)),
+            dma((n_col, chips)),
+            dma((n_col, chips)),
+            dma((n_col, chips)),
             dma((n_col,)),
             dma((n_col,)),
             dma((15,)),
@@ -787,7 +846,7 @@
         moved_order,
         move_destination.reshape(1, move_count),
         move_target.reshape(1, move_count),
-        old_basis.reshape(2, rank_count, source_count),
+        old_basis.reshape(2, chips, row_share, source_count),
         source_nodes,
     )
     scale_factor = math.sqrt(2.0 * node_count * vesicles * n_clu * n_col)

time: 77.9 us -> 71.4 us (0.917)
  Pallas kernels: 77 us -> 70.6 us
    pallas_call x1, Pallas kernels: 72 us -> 65.5 us  [per_device(): pl.pallas_call(functools.partial(main_kernel, sizes), out_shape=(flat_sha...]
where the time goes in v3:
time: 71.4 us; the launch traced here: 71.2 us
  Pallas kernels  70.6 us (99%)
    pallas_call x1, Pallas kernels, per_device(): pl.pallas_call(functools.partial(main_kernel, sizes), out_shape=(flat_sha...  65.5 us
    pallas_call x1, Pallas kernels, per_device(): pl.pallas_call(functools.partial(finish_kernel, scale_factor), out_shape=...  5.08 us

profile of v3, /device:TPU:1, one launch (start us, length us, event | category | flops | bytes accessed | tf_op | source)
XLA Modules:
  0.0 71.2 jit_solution(6171469201023655616)
XLA Ops:
  0.6 65.5 %main_step.1 = (f32[64,128]{1,0:T(8,128)}, f32[64,128]{1,0:T(8,128)}, bf16[128,8192]{1,0:T(8,128)(2,1)}, f32[32,1,128]{2,1,0:T(1,128)}) custom-call(s32[1,32]{1,0:T(1,128)} %bitcast.13, f32[128,256]{1,0:T(8,128)} %constant.2.clone.table_hbm, f32[64,128]{1,0:T(8,128)} %bitcast.11, f32[32,128]{1,0:T(8,128)} %tension_hbm.1, f32[1,32]{1,0:T(1,128)} %bitcast.14, ...), custom_call_target="tpu_custom_call" | custom-call | tf_op jit(solution)/shard_map/main_step/pallas_call | solution.py:780
  66.1 5.1 %finish_step.1 = (f32[32,128,128]{2,1,0:T(8,128)}, f32[64,128]{1,0:T(8,128)}, f32[64,128]{1,0:T(8,128)}) custom-call(f32[32,128]{1,0:T(8,128)} %bitcast.12, bf16[128,8192]{1,0:T(8,128)(2,1)} %get-tuple-element.11.split_in, f32[64,128]{1,0:T(8,128)} %get-tuple-element.12.force_in, f32[64,128]{1,0:T(8,128)} %get-tuple-element.13.near_in), custom_call_target="tpu_custom_call" | custom-call | tf_op jit(solution)/shard_map/finish_step/pallas_call | solution.py:853

commit v4 on v3

--- a/solution.py
+++ b/solution.py
@@ -13,9 +13,9 @@
 HIGHEST = lax.Precision.HIGHEST
 MESH = pl.DeviceIdType.MESH
 CHIPS_X = 4
-LAG = 6
-MOVE_TURN = 12
-DELAY = 4
+LAG = 15
+MOVE_TURN = 13
+DELAY = 1
 ROWS = 8
 VMEM_ALL = 67043328
 
@@ -167,7 +167,147 @@
     own_basis.start()
     load_nodes = pltpu.make_async_copy(nodes_hbm, all_nodes.at[z], own_sem.at[1])
     load_nodes.start()
-    load_nodes.wait()
+    def node_copy(k):
+        return pltpu.make_async_remote_copy(
+            src_ref=nodes_hbm,
+            dst_ref=all_nodes.at[z],
+            send_sem=node_send.at[k],
+            recv_sem=node_recv.at[k],
+            device_id={"col": lax.rem(z + k, n_col)},
+            device_id_type=MESH,
+        )
+
+    def line_offset(turn):
+        odd = lax.rem(turn, 2)
+        return (1 - odd) * (lax.div(turn, 2) + 1) + odd * (n_col - lax.div(turn + 1, 2))
+
+    def peer(down, right):
+        first = lax.rem(minor + down, chips)
+        second = lax.rem(major + right, chips)
+        return {
+            "clu": (first + core * (second - first)) * members
+            + 2 * (second + core * (first - second))
+            + core
+        }
+
+    def tile(ref, row, column):
+        lanes = pl.ds(pl.multiple_of(column * lane_share, lane_share), lane_share)
+        return ref.at[core, row, :, lanes]
+
+    def origin_of(k):
+        return lax.rem(z + n_col - k, n_col)
+
+    def ring_copy(k):
+        return pltpu.make_async_remote_copy(
+            src_ref=tile(basis_ref, major, minor),
+            dst_ref=tile(all_basis.at[z], major, minor),
+            send_sem=ring_send.at[k],
+            recv_sem=ring_recv.at[k],
+            device_id={"col": lax.rem(z + k, n_col)},
+            device_id_type=MESH,
+        )
+
+    def from_ring(k):
+        block = tile(all_basis.at[origin_of(k)], major, minor)
+        return pltpu.make_async_remote_copy(
+            src_ref=block,
+            dst_ref=block,
+            send_sem=ring_send.at[k],
+            recv_sem=ring_recv.at[k],
+            device_id={"col": origin_of(k)},
+            device_id_type=MESH,
+        )
+
+    def first_copy(k, d, back):
+        column = lax.rem(minor + back * (chips - d), chips)
+        block = tile(all_basis.at[origin_of(k)], major, column)
+        return pltpu.make_async_remote_copy(
+            src_ref=block,
+            dst_ref=block,
+            send_sem=first_send.at[k, d],
+            recv_sem=first_recv.at[k, d],
+            device_id=peer(chips - d if back else d, 0),
+            device_id_type=MESH,
+        )
+
+    def second_copy(k, d, back):
+        row = lax.rem(major + back * (chips - d), chips)
+        block = all_basis.at[origin_of(k), core, row]
+        return pltpu.make_async_remote_copy(
+            src_ref=block,
+            dst_ref=block,
+            send_sem=second_send.at[k, d],
+            recv_sem=second_recv.at[k, d],
+            device_id=peer(0, chips - d if back else d),
+            device_id_type=MESH,
+        )
+
+    def pair_copy(k, half):
+        block = all_basis.at[origin_of(k), half]
+        return pltpu.make_async_remote_copy(
+            src_ref=block,
+            dst_ref=block,
+            send_sem=pair_send.at[k],
+            recv_sem=pair_recv.at[k],
+            device_id={"clu": partner},
+            device_id_type=MESH,
+        )
+
+    def service(turn):
+        @pl.when(turn < n_col - 1)
+        def _():
+            k = line_offset(turn)
+            from_ring(k).wait_recv()
+            for d in range(1, chips):
+                first_copy(k, d, 0).start()
+
+        @pl.when((turn >= LAG) & (turn < n_col - 1 + LAG))
+        def _():
+            k = line_offset(turn - LAG)
+            for d in range(1, chips):
+                first_copy(k, d, 1).wait_recv()
+            for d in range(1, chips):
+                second_copy(k, d, 0).start()
+
+        @pl.when(turn >= 2 * LAG)
+        def _():
+            k = line_offset(turn - 2 * LAG)
+            for d in range(1, chips):
+                second_copy(k, d, 1).wait_recv()
+            pair_copy(k, core).start()
+
+    def move_copy(k):
+        other = lax.rem(me + k, n_clu)
+        return pltpu.make_async_remote_copy(
+            src_ref=move_out.at[other],
+            dst_ref=move_in.at[me],
+            send_sem=move_send.at[k],
+            recv_sem=move_recv.at[k],
+            device_id={"clu": other},
+            device_id_type=MESH,
+        )
+
+    def from_peer(buffer, sems_out, sems_in, axis, k, count, index):
+        other = lax.rem(index + count - k, count)
+        return pltpu.make_async_remote_copy(
+            src_ref=buffer.at[other],
+            dst_ref=buffer.at[other],
+            send_sem=sems_out.at[k],
+            recv_sem=sems_in.at[k],
+            device_id={axis: other},
+            device_id_type=MESH,
+        )
+
+    pl.semaphore_wait(barrier, n_clu + n_col - 2)
+
+    @pl.loop(1, n_col)
+    def _(k):
+        node_copy(k).start()
+
+    @pl.loop(0, n_col - 1)
+    def _(turn):
+        ring_copy(line_offset(turn)).start()
+
     for load in loads:
         load.wait()
 
@@ -221,147 +361,6 @@
     move_out[:, 0] = packed.reshape(n_clu, 8, node_count)
     move_out[:, 1] = jnp.broadcast_to(goal, (slot_rows, node_count)).reshape(n_clu, 8, node_count)
 
-    def node_copy(k):
-        return pltpu.make_async_remote_copy(
-            src_ref=nodes_hbm,
-            dst_ref=all_nodes.at[z],
-            send_sem=node_send.at[k],
-            recv_sem=node_recv.at[k],
-            device_id={"col": lax.rem(z + k, n_col)},
-            device_id_type=MESH,
-        )
-
-    def line_offset(turn):
-        odd = lax.rem(turn, 2)
-        return (1 - odd) * (lax.div(turn, 2) + 1) + odd * (n_col - lax.div(turn + 1, 2))
-
-    def peer(down, right):
-        first = lax.rem(minor + down, chips)
-        second = lax.rem(major + right, chips)
-        return {
-            "clu": (first + core * (second - first)) * members
-            + 2 * (second + core * (first - second))
-            + core
-        }
-
-    def tile(ref, row, column):
-        lanes = pl.ds(pl.multiple_of(column * lane_share, lane_share), lane_share)
-        return ref.at[core, row, :, lanes]
-
-    def origin_of(k):
-        return lax.rem(z + n_col - k, n_col)
-
-    def ring_copy(k):
-        return pltpu.make_async_remote_copy(
-            src_ref=tile(basis_ref, major, minor),
-            dst_ref=tile(all_basis.at[z], major, minor),
-            send_sem=ring_send.at[k],
-            recv_sem=ring_recv.at[k],
-            device_id={"col": lax.rem(z + k, n_col)},
-            device_id_type=MESH,
-        )
-
-    def from_ring(k):
-        block = tile(all_basis.at[origin_of(k)], major, minor)
-        return pltpu.make_async_remote_copy(
-            src_ref=block,
-            dst_ref=block,
-            send_sem=ring_send.at[k],
-            recv_sem=ring_recv.at[k],
-            device_id={"col": origin_of(k)},
-            device_id_type=MESH,
-        )
-
-    def first_copy(k, d, back):
-        column = lax.rem(minor + back * (chips - d), chips)
-        block = tile(all_basis.at[origin_of(k)], major, column)
-        return pltpu.make_async_remote_copy(
-            src_ref=block,
-            dst_ref=block,
-            send_sem=first_send.at[k, d],
-            recv_sem=first_recv.at[k, d],
-            device_id=peer(chips - d if back else d, 0),
-            device_id_type=MESH,
-        )
-
-    def second_copy(k, d, back):
-        row = lax.rem(major + back * (chips - d), chips)
-        block = all_basis.at[origin_of(k), core, row]
-        return pltpu.make_async_remote_copy(
-            src_ref=block,
-            dst_ref=block,
-            send_sem=second_send.at[k, d],
-            recv_sem=second_recv.at[k, d],
-            device_id=peer(0, chips - d if back else d),
-            device_id_type=MESH,
-        )
-
-    def pair_copy(k, half):
-        block = all_basis.at[origin_of(k), half]
-        return pltpu.make_async_remote_copy(
-            src_ref=block,
-            dst_ref=block,
-            send_sem=pair_send.at[k],
-            recv_sem=pair_recv.at[k],
-            device_id={"clu": partner},
-            device_id_type=MESH,
-        )
-
-    def service(turn):
-        @pl.when(turn < n_col - 1)
-        def _():
-            k = line_offset(turn)
-            from_ring(k).wait_recv()
-            for d in range(1, chips):
-                first_copy(k, d, 0).start()
-
-        @pl.when((turn >= LAG) & (turn < n_col - 1 + LAG))
-        def _():
-            k = line_offset(turn - LAG)
-            for d in range(1, chips):
-                first_copy(k, d, 1).wait_recv()
-            for d in range(1, chips):
-                second_copy(k, d, 0).start()
-
-        @pl.when(turn >= 2 * LAG)
-        def _():
-            k = line_offset(turn - 2 * LAG)
-            for d in range(1, chips):
-                second_copy(k, d, 1).wait_recv()
-            pair_copy(k, core).start()
-
-    def move_copy(k):
-        other = lax.rem(me + k, n_clu)
-        return pltpu.make_async_remote_copy(
-            src_ref=move_out.at[other],
-            dst_ref=move_in.at[me],
-            send_sem=move_send.at[k],
-            recv_sem=move_recv.at[k],
-            device_id={"clu": other},
-            device_id_type=MESH,
-        )
-
-    def from_peer(buffer, sems_out, sems_in, axis, k, count, index):
-        other = lax.rem(index + count - k, count)
-        return pltpu.make_async_remote_copy(
-            src_ref=buffer.at[other],
-            dst_ref=buffer.at[other],
-            send_sem=sems_out.at[k],
-            recv_sem=sems_in.at[k],
-            device_id={axis: other},
-            device_id_type=MESH,
-        )
-
-    pl.semaphore_wait(barrier, n_clu + n_col - 2)
-
-    @pl.loop(1, n_col)
-    def _(k):
-        node_copy(k).start()
-
-    @pl.loop(0, n_col - 1)
-    def _(turn):
-        ring_copy(line_offset(turn)).start()
-
     services = n_col - 1 + 2 * LAG
     early = n_col - 1 - DELAY
     chunk = 128
@@ -380,17 +379,26 @@
                 turned[:, 1:2], (chunk, node_count)
             )
 
+    load_nodes.wait()
     widen(z)
 
-    @pl.loop(0, n_col - 1)
+    def both_sides(turn, count):
+        for at in range(count):
+            k = line_offset(turn + at)
+            from_peer(all_nodes, node_send, node_recv, "col", k, n_col, z).wait_recv()
+        for at in range(count):
+            widen(origin_of(line_offset(turn + at)))
+        for at in range(count):
+
+            @pl.when(turn + at >= DELAY)
+            def _():
+                service(turn + at - DELAY)
+
+    @pl.loop(0, n_col // 2 - 1)
     def _(turn):
-        k = line_offset(turn)
-        from_peer(all_nodes, node_send, node_recv, "col", k, n_col, z).wait_recv()
-        widen(origin_of(k))
-
-        @pl.when(turn >= DELAY)
-        def _():
-            service(turn - DELAY)
+        both_sides(2 * turn, 2)
+
+    both_sides(n_col - 2, 1)
 
     def form_kernel(b):
         own = far_ref[0, b]
@@ -417,16 +425,21 @@
     own_move.start()
     begun = early
     rounds = vesicles // 2
-    within = min(rounds, services - begun)
+    within = min(2 * rounds, services - begun)
 
     @pl.loop(0, rounds)
     def _(turn):
         form_kernel(2 * turn)
+
+        @pl.when(2 * turn < within)
+        def _():
+            service(begun + 2 * turn)
+
         form_kernel(2 * turn + 1)
 
-        @pl.when(turn < within)
+        @pl.when(2 * turn + 1 < within)
         def _():
-            service(begun + turn)
+            service(begun + 2 * turn + 1)
 
         @pl.when(turn == min(MOVE_TURN, rounds - 1))
         def _():

time: 71.4 us -> 69.9 us (0.979)
  Pallas kernels: 70.6 us -> 69.1 us
    pallas_call x1, Pallas kernels: 65.5 us -> 64 us  [per_device(): pl.pallas_call(functools.partial(main_kernel, sizes), out_shape=(flat_sha...]
where the time goes in v4:
time: 69.9 us; the launch traced here: 69.7 us
  Pallas kernels  69.1 us (99%)
    pallas_call x1, Pallas kernels, per_device(): pl.pallas_call(functools.partial(main_kernel, sizes), out_shape=(flat_sha...  64 us
    pallas_call x1, Pallas kernels, per_device(): pl.pallas_call(functools.partial(finish_kernel, scale_factor), out_shape=...  5.08 us

profile of v4, /device:TPU:1, one launch (start us, length us, event | category | flops | bytes accessed | tf_op | source)
XLA Modules:
  0.0 69.7 jit_solution(5763608289795333355)
XLA Ops:
  0.6 64.0 %main_step.1 = (f32[64,128]{1,0:T(8,128)}, f32[64,128]{1,0:T(8,128)}, bf16[128,8192]{1,0:T(8,128)(2,1)}, f32[32,1,128]{2,1,0:T(1,128)}) custom-call(s32[1,32]{1,0:T(1,128)} %bitcast.13, f32[128,256]{1,0:T(8,128)} %constant.2.clone.table_hbm, f32[64,128]{1,0:T(8,128)} %bitcast.11, f32[32,128]{1,0:T(8,128)} %tension_hbm.1, f32[1,32]{1,0:T(1,128)} %bitcast.14, ...), custom_call_target="tpu_custom_call" | custom-call | tf_op jit(solution)/shard_map/main_step/pallas_call | solution.py:793
  64.6 5.1 %finish_step.1 = (f32[32,128,128]{2,1,0:T(8,128)}, f32[64,128]{1,0:T(8,128)}, f32[64,128]{1,0:T(8,128)}) custom-call(f32[32,128]{1,0:T(8,128)} %bitcast.12, bf16[128,8192]{1,0:T(8,128)(2,1)} %get-tuple-element.11.split_in, f32[64,128]{1,0:T(8,128)} %get-tuple-element.12.force_in, f32[64,128]{1,0:T(8,128)} %get-tuple-element.13.near_in), custom_call_target="tpu_custom_call" | custom-call | tf_op jit(solution)/shard_map/finish_step/pallas_call | solution.py:866
